TPU v7x, 256 devices: a whole 4x4x8 slice. The times are simulated.
256 devices in a mesh: grp: 8 (over y, core), row: 32 (over z, x).
Axes of the slice: x: 4, y: 4, z: 8, core: 2. Of those that a mesh axis runs over, the one named last changes fastest.
Arguments:
- fine_cols: int32 [10240, 5], P(('grp', 'row')), may hold values from 0 to 10239, as said below
- fine_blocks: bfloat16 [10240, 5, 128, 128], P(('grp', 'row'))
- prolong_cols: int32 [10240, 2], replicated, may hold values from 0 to 1023, as said below
- prolong_blocks: bfloat16 [10240, 2, 128, 128], P(('grp', 'row')), may hold values from -0.125 to 0.125
- agg_owner: int32 [1024], replicated, may hold values from 0 to 7, as said below
- coarse_rhs: float32 [1024, 128], P(('grp', 'row')), may hold values from -6 to 6
- lam_low: float32 [1], replicated, may hold values from 0.05 to 0.5
- lam_high: float32 [1], replicated, may hold values from 1.5 to 3.5
Outputs:
- coarse_operator: float32 [2048, 7, 128, 128], P(('grp', 'row'))
- coarse_solution: float32 [2048, 128], P(('grp', 'row'))
- coarse_residual: float32 [2048, 128], P(('grp', 'row'))
Inputs may be any that keep to these rules, and one draw needn't show every extreme that they name: fine_cols[i, 0] = i; the other 4 entries of row i are distinct rows (i + t) mod 10240 with 1 <= |t| <= 10; some row reaches |t| = 10. `prolong_cols`: the two entries of fine row i are two distinct ones of i // 10 - 1, i // 10, i // 10 + 1 in rising order, taken modulo 1024. `agg_owner`: the 4 aggregates made on one device go to distinct groups; for every row index some group owns one aggregate from each of the 8 groups at that row index.
All inputs are finite; a program needn't handle non-finite values.
Results may differ from a plain program's by a relative error of at most 0.0019.
Values may be sent and summed in bfloat16 or wider, within the bound.
A program may use at most 128 MiB of HBM per device.

v0:
```python
import jax
import jax.numpy as jnp
from jax import lax
from jax.sharding import PartitionSpec as P

HIGH = lax.Precision.HIGHEST


def extended_2(block, sides, width):
    for axis, dim in sides:
        count = lax.axis_size(axis)
        forward = [(i, i + 1) for i in range(count - 1)]
        forward.append((count - 1, 0))
        backward = [(target, source) for source, target in forward]
        low = lax.ppermute(
            lax.slice_in_dim(block, block.shape[dim] - width, None, axis=dim), axis, forward
        )
        high = lax.ppermute(lax.slice_in_dim(block, 0, width, axis=dim), axis, backward)
        block = jnp.concatenate([low, block, high], axis=dim)
    return block


def chebyshev_terms(lam_low, lam_high):
    center = 0.5 * (lam_high[0] + lam_low[0])
    radius = 0.5 * (lam_high[0] - lam_low[0])
    sigma_ratio = center / radius
    first_rho = 1.0 / sigma_ratio
    second_rho = 1.0 / (2.0 * sigma_ratio - first_rho)
    return (center, second_rho * first_rho, 2.0 * second_rho / radius)


def per_device(
    fine_cols, fine_blocks, prolong_cols, prolong_blocks, agg_owner, coarse_rhs, lam_low, lam_high
):
    rows_dev = fine_blocks.shape[0]
    band_width = fine_blocks.shape[2]
    groups = lax.axis_size("grp")
    rows_axis = lax.axis_size("row")
    devices = groups * rows_axis
    aggs_dev = coarse_rhs.shape[0]
    agg_rows = rows_dev // aggs_dev
    fine_total = rows_dev * devices
    coarse_total = aggs_dev * devices
    my_grp = lax.axis_index("grp")
    my_row = lax.axis_index("row")
    device = my_grp * rows_axis + my_row
    first_row = device * rows_dev
    offsets = jnp.arange(-2, 3, dtype=jnp.int32)
    group_ids = jnp.arange(groups, dtype=jnp.int32)
    p_pad = extended_2(prolong_blocks, ((("grp", "row"), 0),), agg_rows)
    pad_ids = (
        first_row - agg_rows + jnp.arange(rows_dev + 2 * agg_rows, dtype=jnp.int32)
    ) % fine_total
    cols_pad = jnp.take(prolong_cols, pad_ids, axis=0)

    def one_aggregate(agg_index):
        start = agg_index * agg_rows
        block_a = lax.dynamic_slice_in_dim(fine_blocks, start, agg_rows, 0)
        cols_here = lax.dynamic_slice_in_dim(fine_cols, start, agg_rows, 0)
        local_rows = start + jnp.arange(agg_rows, dtype=jnp.int32)
        global_rows = first_row + local_rows
        reach = (cols_here - global_rows[:, None] + agg_rows) % fine_total - agg_rows
        positions = local_rows[:, None] + agg_rows + reach
        p_near = jnp.take(p_pad, positions, axis=0)
        near_cols = jnp.take(cols_pad, positions, axis=0)
        agg_id = device * aggs_dev + agg_index
        shifted = (near_cols - agg_id + 2) % coarse_total - 2
        chosen = (shifted[..., None] == offsets).astype(jnp.float32)
        products = jnp.einsum(
            "iakm,iaqmn->iaqkn", block_a, p_near, preferred_element_type=jnp.float32
        )
        merged = jnp.einsum("iaqo,iaqkn->iokn", chosen, products, precision=HIGH).astype(
            jnp.bfloat16
        )
        own_blocks = lax.dynamic_slice_in_dim(prolong_blocks, start, agg_rows, 0)
        own_cols = lax.dynamic_slice_in_dim(cols_pad, start + agg_rows, agg_rows, 0)
        step_off = (own_cols - agg_id + 1) % coarse_total - 1
        term_blocks = jnp.einsum(
            "ipmk,iomn->ipokn", own_blocks, merged, preferred_element_type=jnp.float32
        )
        lifted = step_off[:, :, None, None, None]
        placing = (
            (lifted + 1 == jnp.arange(3, dtype=jnp.int32)[:, None])
            & (offsets[None, None, :, None, None] - lifted + 3 == jnp.arange(7, dtype=jnp.int32))
        ).astype(jnp.float32)
        return jnp.einsum("ipots,ipokn->tskn", placing, term_blocks, precision=HIGH)

    pieces = lax.map(one_aggregate, jnp.arange(aggs_dev, dtype=jnp.int32))
    partial_value = jnp.zeros((aggs_dev + 2, 7, band_width, band_width), jnp.float32)
    for target in range(3):
        partial_value = partial_value.at[target : target + aggs_dev].add(pieces[:, target])
    owners_mine = lax.dynamic_slice_in_dim(agg_owner, device * aggs_dev, aggs_dev, 0)
    send_onehot = (owners_mine[:, None] == group_ids).astype(jnp.float32)
    send_rhs = jnp.einsum("kg,kn->gn", send_onehot, coarse_rhs, precision=HIGH)
    extended = extended_2(partial_value, ((("grp", "row"), 0),), 1)
    native = partial_value[1 : aggs_dev + 1]
    native = native.at[0].add(extended[0])
    native = native.at[aggs_dev - 1].add(extended[aggs_dev + 3])
    send_rows = jnp.einsum("kg,ksmn->gsmn", send_onehot, native, precision=HIGH)
    got_rows, got_rhs = (
        lax.all_to_all(send_rows, "grp", split_axis=0, concat_axis=0, tiled=True),
        lax.all_to_all(send_rhs, "grp", split_axis=0, concat_axis=0, tiled=True),
    )
    source_dev = group_ids * rows_axis + my_row
    agg_table = source_dev[:, None] * aggs_dev + jnp.arange(aggs_dev, dtype=jnp.int32)
    matches = (jnp.take(agg_owner, agg_table, axis=0) == my_grp).astype(jnp.int32)
    slot_agg = source_dev * aggs_dev + jnp.sum(
        matches * jnp.arange(aggs_dev, dtype=jnp.int32), axis=1
    )
    near_ids = (slot_agg[:, None] + jnp.arange(7, dtype=jnp.int32) - 3) % coarse_total
    near_dev = near_ids // aggs_dev
    near_grp = near_dev // rows_axis
    near_row = near_dev % rows_axis
    near_owner = jnp.take(agg_owner, near_ids, axis=0)

    def operate(vector):
        whole = lax.all_gather(vector, ("grp", "row"), axis=0, tiled=True)
        nearby = jnp.take(whole, (near_owner * rows_axis + near_row) * groups + near_grp, axis=0)
        return jnp.einsum("gsmn,gsn->gm", got_rows, nearby, precision=HIGH)

    center, old_weight, resid_weight = chebyshev_terms(lam_low, lam_high)
    first_iter = got_rhs / center
    first_resid = got_rhs - operate(first_iter)
    second_iter = first_iter + old_weight * first_iter + resid_weight * first_resid
    second_resid = got_rhs - operate(second_iter)
    return (got_rows, second_iter, second_resid)


def solution(mesh):
    return jax.shard_map(
        per_device,
        mesh=mesh,
        in_specs=(
            P(("grp", "row"), None),
            P(("grp", "row"), None, None, None),
            P(),
            P(("grp", "row"), None, None, None),
            P(),
            P(("grp", "row"), None),
            P(),
            P(),
        ),
        out_specs=(
            P(("grp", "row"), None, None, None),
            P(("grp", "row"), None),
            P(("grp", "row"), None),
        ),
        check_vma=False,
    )
```

profile of v0, /device:TPU:1, one launch (start us, length us, event | category | flops | bytes accessed | tf_op | source)
XLA Modules:
  0.0 583.9 jit_solution(10987784176769533986)
XLA Ops:
  11.5 7.1 %collective-permute-start.1 = (bf16[10,2,128,128]{3,2,1,0:T(8,128)(2,1)S(1)}, bf16[10,2,128,128]{3,2,1,0:T(8,128)(2,1)}, u32[]{:S(2)}, u32[]{:S(2)}) collective-permute-start(bf16[10,2,128,128]{3,2,1,0:T(8,128)(2,1)S(1)} %get-tuple-element.460), channel_id=1, source_target_pairs={{1,0},{2,1},{3,2},{4,3},{5,4},{6,5},{7,6},{8,7},{9,8},{10,9},{11,1... | collective-permute-start | bytes 1966088 | tf_op jit(solution)/shard_map/ppermute | solution.py:18
  18.6 3.9 copy.53
  22.5 3.1 gather_fusion.2
  25.8 7.8 %collective-permute-done = bf16[10,2,128,128]{3,2,1,0:T(8,128)(2,1)} collective-permute-done((bf16[10,2,128,128]{3,2,1,0:T(8,128)(2,1)}, bf16[10,2,128,128]{3,2,1,0:T(8,128)(2,1)}, u32[]{:S(2)}, u32[]{:S(2)}) %collective-permute-start) | collective-permute-done | bytes 655392 | tf_op jit(solution)/shard_map/ppermute | solution.py:15
  33.6 3.3 pad_maximum_fusion
  36.9 265.3 %while.22 = (s32[]{:T(128)}, f32[4,3,7,128,128]{4,2,3,1,0:T(8,128)}, s32[4]{0:T(128)S(1)}, s32[60,2]{0,1:T(2,128)S(1)}, s32[]{:T(128)}, /*index=5*/s32[40,5]{0,1...) while((s32[]{:T(128)}, ...), condition=%wide.region_1.2_spmd.clone.clone, body=%wide.region_0.1_spmd.clone.clone.sunk | while | flops 1352506368 | bytes 91372768 | solution.py:88
  38.7 4.9 gather_fusion
  43.6 4.3 copy.98
  47.8 5.2 fusion.101
  53.0 10.1 %copy.99 = f32[10,5,2,128,128]{4,1,2,3,0:T(8,128)} copy(f32[10,5,2,128,128]{3,4,2,1,0:T(8,128)} %fusion.101) | data formatting | bytes 13107200 | tf_op jit(solution)/shard_map/while/body/eval_jaxpr/iakm,iaqmn->iaqkn/transpose | solution.py:69
  64.8 10.6 %fusion.103 = bf16[10,5,128,128,1]{3,1,2,0,4:T(8,128)(2,1)S(1)} fusion(f32[10,5,2,128,128]{4,1,2,3,0:T(8,128)} %copy.99, s32[10,5,2]{1,2,0:T(2,128)S(1)} %copy.102, s32[5]{0:T(128)S(1)} %iota_add_fusion.3), kind=kOutput, calls=%fused_computation.16.clone.1 | convolution fusion | flops 99123696 | bytes 8192420 | tf_op jit(solution)/shard_map/while/body/eval_jaxpr/iaqo,iaqkn->iokn/dot_general | solution.py:72
  75.4 3.8 convolution_bitcast_fusion.2
  79.2 11.5 %copy.103 = f32[10,2,5,128,128]{4,0,1,2,3:T(8,128)} copy(f32[10,2,5,128,128]{3,4,1,2,0:T(8,128)} %convolution_bitcast_fusion.2) | data formatting | bytes 13107200 | tf_op jit(solution)/shard_map/while/body/eval_jaxpr/ipmk,iomn->ipokn/transpose | solution.py:78
  90.9 12.4 %bitcast_dynamic-update-slice_fusion.2 = f32[4,3,7,128,128]{4,2,3,1,0:T(8,128)} fusion(f32[4,3,7,128,128]{4,2,3,1,0:T(8,128)} %get-tuple-element.550, s32[]{:T(128)} %get-tuple-element.549, f32[10,2,5,128,128]{4,0,1,2,3:T(8,128)} %copy.103, pred[10,2,5,7]{0,3,1,2:T(8,128)(4,1)S(1)} %iota_compare_fusion.6, pred[10,2,3]{0,1,2:T(4,128)(4,1)S(1)} %iota_compare_fusion.7), kind=kOutput, calls=%fused_computation.21.clone.1 | convolution fusion | flops 412878912 | bytes 12059896 | tf_op jit(solution)/shard_map/while/body/eval_jaxpr/ipots,ipokn->tskn/dot_general | solution.py:86
  105.0 4.9 gather_fusion
  109.9 4.3 copy.98
  114.2 5.2 fusion.101
  119.4 10.1 %copy.99 = f32[10,5,2,128,128]{4,1,2,3,0:T(8,128)} copy(f32[10,5,2,128,128]{3,4,2,1,0:T(8,128)} %fusion.101) | data formatting | bytes 13107200 | tf_op jit(solution)/shard_map/while/body/eval_jaxpr/iakm,iaqmn->iaqkn/transpose | solution.py:69
  131.1 10.6 %fusion.103 = bf16[10,5,128,128,1]{3,1,2,0,4:T(8,128)(2,1)S(1)} fusion(f32[10,5,2,128,128]{4,1,2,3,0:T(8,128)} %copy.99, s32[10,5,2]{1,2,0:T(2,128)S(1)} %copy.102, s32[5]{0:T(128)S(1)} %iota_add_fusion.3), kind=kOutput, calls=%fused_computation.16.clone.1 | convolution fusion | flops 99123696 | bytes 8192420 | tf_op jit(solution)/shard_map/while/body/eval_jaxpr/iaqo,iaqkn->iokn/dot_general | solution.py:72
  141.8 3.8 convolution_bitcast_fusion.2
  145.5 11.5 %copy.103 = f32[10,2,5,128,128]{4,0,1,2,3:T(8,128)} copy(f32[10,2,5,128,128]{3,4,1,2,0:T(8,128)} %convolution_bitcast_fusion.2) | data formatting | bytes 13107200 | tf_op jit(solution)/shard_map/while/body/eval_jaxpr/ipmk,iomn->ipokn/transpose | solution.py:78
  157.2 12.4 %bitcast_dynamic-update-slice_fusion.2 = f32[4,3,7,128,128]{4,2,3,1,0:T(8,128)} fusion(f32[4,3,7,128,128]{4,2,3,1,0:T(8,128)} %get-tuple-element.550, s32[]{:T(128)} %get-tuple-element.549, f32[10,2,5,128,128]{4,0,1,2,3:T(8,128)} %copy.103, pred[10,2,5,7]{0,3,1,2:T(8,128)(4,1)S(1)} %iota_compare_fusion.6, pred[10,2,3]{0,1,2:T(4,128)(4,1)S(1)} %iota_compare_fusion.7), kind=kOutput, calls=%fused_computation.21.clone.1 | convolution fusion | flops 412878912 | bytes 12059896 | tf_op jit(solution)/shard_map/while/body/eval_jaxpr/ipots,ipokn->tskn/dot_general | solution.py:86
  171.3 4.9 gather_fusion
  176.2 4.3 copy.98
  180.5 5.2 fusion.101
  185.7 10.1 %copy.99 = f32[10,5,2,128,128]{4,1,2,3,0:T(8,128)} copy(f32[10,5,2,128,128]{3,4,2,1,0:T(8,128)} %fusion.101) | data formatting | bytes 13107200 | tf_op jit(solution)/shard_map/while/body/eval_jaxpr/iakm,iaqmn->iaqkn/transpose | solution.py:69
  197.4 10.6 %fusion.103 = bf16[10,5,128,128,1]{3,1,2,0,4:T(8,128)(2,1)S(1)} fusion(f32[10,5,2,128,128]{4,1,2,3,0:T(8,128)} %copy.99, s32[10,5,2]{1,2,0:T(2,128)S(1)} %copy.102, s32[5]{0:T(128)S(1)} %iota_add_fusion.3), kind=kOutput, calls=%fused_computation.16.clone.1 | convolution fusion | flops 99123696 | bytes 8192420 | tf_op jit(solution)/shard_map/while/body/eval_jaxpr/iaqo,iaqkn->iokn/dot_general | solution.py:72
  208.1 3.8 convolution_bitcast_fusion.2
  211.8 11.5 %copy.103 = f32[10,2,5,128,128]{4,0,1,2,3:T(8,128)} copy(f32[10,2,5,128,128]{3,4,1,2,0:T(8,128)} %convolution_bitcast_fusion.2) | data formatting | bytes 13107200 | tf_op jit(solution)/shard_map/while/body/eval_jaxpr/ipmk,iomn->ipokn/transpose | solution.py:78
  223.5 12.4 %bitcast_dynamic-update-slice_fusion.2 = f32[4,3,7,128,128]{4,2,3,1,0:T(8,128)} fusion(f32[4,3,7,128,128]{4,2,3,1,0:T(8,128)} %get-tuple-element.550, s32[]{:T(128)} %get-tuple-element.549, f32[10,2,5,128,128]{4,0,1,2,3:T(8,128)} %copy.103, pred[10,2,5,7]{0,3,1,2:T(8,128)(4,1)S(1)} %iota_compare_fusion.6, pred[10,2,3]{0,1,2:T(4,128)(4,1)S(1)} %iota_compare_fusion.7), kind=kOutput, calls=%fused_computation.21.clone.1 | convolution fusion | flops 412878912 | bytes 12059896 | tf_op jit(solution)/shard_map/while/body/eval_jaxpr/ipots,ipokn->tskn/dot_general | solution.py:86
  237.6 4.9 gather_fusion
  242.5 4.3 copy.98
  246.7 5.2 fusion.101
  252.0 10.1 %copy.99 = f32[10,5,2,128,128]{4,1,2,3,0:T(8,128)} copy(f32[10,5,2,128,128]{3,4,2,1,0:T(8,128)} %fusion.101) | data formatting | bytes 13107200 | tf_op jit(solution)/shard_map/while/body/eval_jaxpr/iakm,iaqmn->iaqkn/transpose | solution.py:69
  263.7 10.6 %fusion.103 = bf16[10,5,128,128,1]{3,1,2,0,4:T(8,128)(2,1)S(1)} fusion(f32[10,5,2,128,128]{4,1,2,3,0:T(8,128)} %copy.99, s32[10,5,2]{1,2,0:T(2,128)S(1)} %copy.102, s32[5]{0:T(128)S(1)} %iota_add_fusion.3), kind=kOutput, calls=%fused_computation.16.clone.1 | convolution fusion | flops 99123696 | bytes 8192420 | tf_op jit(solution)/shard_map/while/body/eval_jaxpr/iaqo,iaqkn->iokn/dot_general | solution.py:72
  274.3 3.8 convolution_bitcast_fusion.2
  278.1 11.5 %copy.103 = f32[10,2,5,128,128]{4,0,1,2,3:T(8,128)} copy(f32[10,2,5,128,128]{3,4,1,2,0:T(8,128)} %convolution_bitcast_fusion.2) | data formatting | bytes 13107200 | tf_op jit(solution)/shard_map/while/body/eval_jaxpr/ipmk,iomn->ipokn/transpose | solution.py:78
  289.8 12.4 %bitcast_dynamic-update-slice_fusion.2 = f32[4,3,7,128,128]{4,2,3,1,0:T(8,128)} fusion(f32[4,3,7,128,128]{4,2,3,1,0:T(8,128)} %get-tuple-element.550, s32[]{:T(128)} %get-tuple-element.549, f32[10,2,5,128,128]{4,0,1,2,3:T(8,128)} %copy.103, pred[10,2,5,7]{0,3,1,2:T(8,128)(4,1)S(1)} %iota_compare_fusion.6, pred[10,2,3]{0,1,2:T(4,128)(4,1)S(1)} %iota_compare_fusion.7), kind=kOutput, calls=%fused_computation.21.clone.1 | convolution fusion | flops 412878912 | bytes 12059896 | tf_op jit(solution)/shard_map/while/body/eval_jaxpr/ipots,ipokn->tskn/dot_general | solution.py:86
  306.8 17.2 %collective-permute-done.2 = f32[1,7,128,128]{3,1,2,0:T(8,128)S(1)} collective-permute-done((f32[1,7,128,128]{3,1,2,0:T(8,128)S(1)}, f32[1,7,128,128]{3,1,2,0:T(8,128)S(1)}, u32[]{:S(2)}, u32[]{:S(2)}) %collective-permute-start.2) | collective-permute-done | bytes 458784 | tf_op jit(solution)/shard_map/ppermute | solution.py:15
  325.2 6.8 %all-to-all-start.1 = ((f32[8,1,128]{2,1,0:T(1,128)}), f32[8,1,128]{2,1,0:T(1,128)S(1)}, u32[]{:S(2)}, u32[]{:S(2)}) async-start(f32[8,1,128]{2,1,0:T(1,128)} %bitcast.7), calls=%async_computation.1 | async-start | bytes 8192 | tf_op jit(solution)/shard_map/all_to_all | solution.py:102
  334.5 3.4 fusion.42
  337.9 2.5 copy.59
  340.4 9.1 %all-to-all-start = ((f32[8,7,128,128]{3,2,1,0:T(8,128)}), f32[8,7,128,128]{3,2,1,0:T(8,128)}, u32[]{:S(2)}, u32[]{:S(2)}) async-start(f32[8,7,128,128]{3,2,1,0:T(8,128)} %copy.59), calls=%async_computation | async-start | bytes 7340032 | tf_op jit(solution)/shard_map/all_to_all | solution.py:101
  354.2 101.2 %all-gather.3.cloned.1.call-done = f32[2048,128]{1,0:T(8,128)} async-done(((f32[8,128]{1,0:T(8,128)}), f32[2048,128]{1,0:T(8,128)}) %all-gather.3.cloned.1.call-update) | async-done | bytes 1048592 | tf_op jit(solution)/shard_map/all_gather | solution.py:117
  457.3 5.5 fusion.48
  463.5 101.2 %all-gather.5.cloned.1.call-done = f32[2048,128]{1,0:T(8,128)} async-done(((f32[8,128]{1,0:T(8,128)}), f32[2048,128]{1,0:T(8,128)}) %all-gather.5.cloned.1.call-update) | async-done | bytes 1048592 | tf_op jit(solution)/shard_map/all_gather | solution.py:117
  566.6 5.6 fusion.46
  572.7 4.3 copy.118
  (145 shorter events, 29.3 us)
Async XLA Ops:
  7.2 317.2 %copy-start = (f32[4,128]{1,0:T(4,128)S(1)}, f32[4,128]{1,0:T(4,128)}, u32[]{:S(2)}) copy-start(f32[4,128]{1,0:T(4,128)} %param.27) | copy-start | bytes 6148
  9.4 24.2 %copy-start.2 = (bf16[40,2,128,128]{3,2,1,0:T(8,128)(2,1)S(1)}, bf16[40,2,128,128]{3,2,1,0:T(8,128)(2,1)}, u32[]{:S(2)}) copy-start(bf16[40,2,128,128]{3,2,1,0:T(8,128)(2,1)} %param.25) | copy-start | bytes 7864324
  9.4 24.2 %collective-permute-start = (bf16[10,2,128,128]{3,2,1,0:T(8,128)(2,1)}, bf16[10,2,128,128]{3,2,1,0:T(8,128)(2,1)}, u32[]{:S(2)}, u32[]{:S(2)}) collective-permute-start(bf16[10,2,128,128]{3,2,1,0:T(8,128)(2,1)} %get-tuple-element.459), channel_id=1, source_target_pairs={{0,1},{1,2},{2,3},{3,4},{4,5},{5,6},{6,7},{7,8},{8,9},{9,10},{10,1... | collective-permute-start | bytes 1966088 | tf_op jit(solution)/shard_map/ppermute | solution.py:15
  11.5 22.2 %collective-permute-start.1 = (bf16[10,2,128,128]{3,2,1,0:T(8,128)(2,1)S(1)}, bf16[10,2,128,128]{3,2,1,0:T(8,128)(2,1)}, u32[]{:S(2)}, u32[]{:S(2)}) collective-permute-start(bf16[10,2,128,128]{3,2,1,0:T(8,128)(2,1)S(1)} %get-tuple-element.460), channel_id=1, source_target_pairs={{1,0},{2,1},{3,2},{4,3},{5,4},{6,5},{7,6},{8,7},{9,8},{10,9},{11,1... | collective-permute-start | bytes 1966088 | tf_op jit(solution)/shard_map/ppermute | solution.py:18
  25.8 11.1 %copy-start.5 = (s32[40,5]{0,1:T(8,128)S(1)}, s32[40,5]{0,1:T(8,128)}, u32[]{:S(2)}) copy-start(s32[40,5]{0,1:T(8,128)} %param.22) | copy-start | bytes 2404
  64.8 10.6 %copy-start.3 = (bf16[40,2,128,128]{3,2,1,0:T(8,128)(2,1)S(1)}, bf16[40,2,128,128]{3,2,1,0:T(8,128)(2,1)}, u32[]{:S(2)}) copy-start(bf16[40,2,128,128]{3,2,1,0:T(8,128)(2,1)} %get-tuple-element.602) | copy-start | bytes 7864324 | tf_op jit(solution)/shard_map/while
  131.1 10.6 %copy-start.3 = (bf16[40,2,128,128]{3,2,1,0:T(8,128)(2,1)S(1)}, bf16[40,2,128,128]{3,2,1,0:T(8,128)(2,1)}, u32[]{:S(2)}) copy-start(bf16[40,2,128,128]{3,2,1,0:T(8,128)(2,1)} %get-tuple-element.602) | copy-start | bytes 7864324 | tf_op jit(solution)/shard_map/while
  197.4 10.6 %copy-start.3 = (bf16[40,2,128,128]{3,2,1,0:T(8,128)(2,1)S(1)}, bf16[40,2,128,128]{3,2,1,0:T(8,128)(2,1)}, u32[]{:S(2)}) copy-start(bf16[40,2,128,128]{3,2,1,0:T(8,128)(2,1)} %get-tuple-element.602) | copy-start | bytes 7864324 | tf_op jit(solution)/shard_map/while
  263.7 10.6 %copy-start.3 = (bf16[40,2,128,128]{3,2,1,0:T(8,128)(2,1)S(1)}, bf16[40,2,128,128]{3,2,1,0:T(8,128)(2,1)}, u32[]{:S(2)}) copy-start(bf16[40,2,128,128]{3,2,1,0:T(8,128)(2,1)} %get-tuple-element.602) | copy-start | bytes 7864324 | tf_op jit(solution)/shard_map/while
  302.2 3.4 copy-start.4
  306.4 17.6 %collective-permute-start.2 = (f32[1,7,128,128]{3,1,2,0:T(8,128)S(1)}, f32[1,7,128,128]{3,1,2,0:T(8,128)S(1)}, u32[]{:S(2)}, u32[]{:S(2)}) collective-permute-start(f32[1,7,128,128]{3,1,2,0:T(8,128)S(1)} %slice.195), channel_id=1, source_target_pairs={{0,1},{1,2},{2,3},{3,4},{4,5},{5,6},{6,7},{7,8},{8,9},{9,10},{10,1... | collective-permute-start | bytes 1376264 | tf_op jit(solution)/shard_map/ppermute | solution.py:15
  306.6 17.7 %copy-start.1 = (s32[1024]{0:T(1024)S(1)}, s32[1024]{0:T(1024)}, u32[]{:S(2)}) copy-start(s32[1024]{0:T(1024)} %param.26) | copy-start | bytes 12292
  324.2 10.2 %collective-permute-start.3 = (f32[1,7,128,128]{3,1,2,0:T(8,128)S(1)}, f32[1,7,128,128]{3,1,2,0:T(8,128)S(1)}, u32[]{:S(2)}, u32[]{:S(2)}) collective-permute-start(f32[1,7,128,128]{3,1,2,0:T(8,128)S(1)} %get-tuple-element.457), channel_id=1, source_target_pairs={{1,0},{2,1},{3,2},{4,3},{5,4},{6,5},{7,6},{8,7},{9,8},{10,9},{11,1... | collective-permute-start | bytes 1376264 | tf_op jit(solution)/shard_map/ppermute | solution.py:18
  325.2 15.2 %all-to-all-start.1 = ((f32[8,1,128]{2,1,0:T(1,128)}), f32[8,1,128]{2,1,0:T(1,128)S(1)}, u32[]{:S(2)}, u32[]{:S(2)}) async-start(f32[8,1,128]{2,1,0:T(1,128)} %bitcast.7), calls=%async_computation.1 | async-start | bytes 8192 | tf_op jit(solution)/shard_map/all_to_all | solution.py:102
  340.4 117.0 %all-to-all-start = ((f32[8,7,128,128]{3,2,1,0:T(8,128)}), f32[8,7,128,128]{3,2,1,0:T(8,128)}, u32[]{:S(2)}, u32[]{:S(2)}) async-start(f32[8,7,128,128]{3,2,1,0:T(8,128)} %copy.59), calls=%async_computation | async-start | bytes 7340032 | tf_op jit(solution)/shard_map/all_to_all | solution.py:101
  349.5 106.0 %all-gather.3.cloned.1.call-start = ((), (), s32[]{:S(2)}) async-start(), calls=%async_computation.2 | async-start | bytes 1052672 | tf_op jit(solution)/shard_map/all_gather | solution.py:117
  351.4 213.3 %all-gather.5.cloned.1.call-start = ((), (), s32[]{:S(2)}) async-start(), calls=%async_computation.3 | async-start | bytes 1052672 | tf_op jit(solution)/shard_map/all_gather | solution.py:117
Sparse Core Ops, SparseCore 0:
  354.6 100.7 all-gather.2
  463.6 100.9 all-gather.4
where the time goes:
time: 587 us; the launch traced here: 584 us
  waiting for transfers between devices  230 us (39%)
  local copies, waits for them, and re-layouts  156 us (27%)
  matrix products  143 us (24%)
  starting transfers between devices  25.5 us (4%)
  between operations  15.7 us (3%)
  other arithmetic  8.03 us (1%)
  loops' own time  5.94 us (1%)
    all_gather x2, waiting for transfers between devices, operate(): whole = lax.all_gather(vector, ('grp', 'row'), axis=0, tiled=True)  202 us
    dot_general x4, matrix products, one_aggregate(): return jnp.einsum('ipots,ipokn->tskn', placing, term_blocks, precision=HIGH)  49.6 us
    transpose x4, local copies, waits for them, and re-layouts, one_aggregate(): jnp.einsum('ipmk,iomn->ipokn', own_blocks, merged, preferred_element_type...  45.9 us
    dot_general x4, matrix products, one_aggregate(): jnp.einsum('iaqo,iaqkn->iokn', chosen, products, precision=HIGH)  42.5 us
    transpose x4, local copies, waits for them, and re-layouts, one_aggregate(): jnp.einsum('iakm,iaqmn->iaqkn', block_a, p_near, preferred_element_type=j...  40.5 us
    gather x8, local copies, waits for them, and re-layouts, one_aggregate(): p_near = jnp.take(p_pad, positions, axis=0)  36.6 us
    ppermute x2, waiting for transfers between devices, extended_2(): lax.ppermute(lax.slice_in_dim(block, block.shape[dim] - width, None, axis...  25.1 us
    dot_general x4, matrix products, one_aggregate(): jnp.einsum('iakm,iaqmn->iaqkn', block_a, p_near, preferred_element_type=j...  20.8 us
  transfers between devices with their start and end apart: 8, of which 5 were waited for; matrix products, arithmetic and copies ran while one was open for 3% of the time, Pallas kernels for 0%

commit v1 on v0

v1 whole, which is shorter than its diff:
```python
import functools

import jax
import jax.numpy as jnp
from jax import lax
from jax.experimental import pallas as pl
from jax.experimental.pallas import tpu as pltpu
from jax.sharding import PartitionSpec as P

MESH = pl.DeviceIdType.MESH
BLK = 128
AGG = 10
AGGS = 4
ROWS = AGG * AGGS
F32 = jnp.float32
BF16 = jnp.bfloat16
Q_MAX = 32767.0
TINY = 2.0**-110


def chebyshev_terms(lam_low, lam_high):
    center = 0.5 * (lam_high[0] + lam_low[0])
    radius = 0.5 * (lam_high[0] - lam_low[0])
    sigma_ratio = center / radius
    first_rho = 1.0 / sigma_ratio
    second_rho = 1.0 / (2.0 * sigma_ratio - first_rho)
    return (center, second_rho * first_rho, 2.0 * second_rho / radius)


def quantised(block):
    top = jnp.maximum(jnp.max(jnp.abs(block), axis=0, keepdims=True), TINY)
    q = jnp.floor(block * (Q_MAX / top) + 0.5).astype(jnp.int32).astype(jnp.int16)
    return q, top * (1.0 / Q_MAX)


def kernel(
    groups, rows_axis,
    tbl, sel, par, a_hbm, p_hbm, rhs_ref,
    q_out, sc_out, xr_out,
    a_v, p_v, h_lo, h_hi, pt, m_v, acc_lo, acc_hi, co, qb, sb, sq, ss, xrb, sx,
    pq_s, ps_s, pq_r, ps_r, own, halo_x, own2, halo_x2,
    a_sem, p_sem, nb_send, nb_recv, gq_send, gq_recv, gs_send, gs_recv, gx_send, gx_recv, self_sem,
):
    g = lax.axis_index("grp")
    r = lax.axis_index("row")
    last = (r + 1) // rows_axis
    nxt = ((g + last) % groups, (r + 1) % rows_axis)
    first = (rows_axis - r) // rows_axis
    prv = ((g + groups - first) % groups, (r + rows_axis - 1) % rows_axis)

    a_copies = [
        pltpu.make_async_copy(a_hbm.at[pl.ds(k * AGG, AGG)], a_v.at[pl.ds(k * AGG, AGG)], a_sem.at[k])
        for k in range(AGGS)
    ]
    p_copy = pltpu.make_async_copy(p_hbm, p_v.at[pl.ds(0, 2 * ROWS)], p_sem)
    p_copy.start()
    for k in (1, 2, 0, 3):
        a_copies[k].start()

    zero_block = jnp.zeros((BLK, BLK), BF16)
    p_v[2 * ROWS] = zero_block
    h_lo[2 * AGG] = zero_block
    h_hi[2 * AGG] = zero_block
    own[...] = jnp.zeros_like(own)
    own[0:AGGS, :] = rhs_ref[...]

    barrier = pltpu.get_barrier_semaphore()
    for target in (nxt, prv):
        pl.semaphore_signal(barrier, inc=1, device_id=target, device_id_type=MESH)
    for off in range(1, groups):
        pl.semaphore_signal(barrier, inc=1, device_id=((g + off) % groups, r), device_id_type=MESH)
    pl.semaphore_wait(barrier, groups + 1)

    def to_neighbour(slot, src, dst, target):
        return pltpu.make_async_remote_copy(
            src_ref=src, dst_ref=dst, send_sem=nb_send.at[slot], recv_sem=nb_recv.at[slot],
            device_id=target, device_id_type=MESH)

    p_next = to_neighbour(0, p_hbm.at[pl.ds(2 * (ROWS - AGG), 2 * AGG)], h_lo.at[pl.ds(0, 2 * AGG)], nxt)
    p_prev = to_neighbour(1, p_hbm.at[pl.ds(0, 2 * AGG)], h_hi.at[pl.ds(0, 2 * AGG)], prv)
    p_next.start()
    p_prev.start()
    x_next = to_neighbour(2, own, halo_x.at[0], nxt)
    x_prev = to_neighbour(3, own, halo_x.at[1], prv)
    x_next.start()
    x_prev.start()

    co[...] = jnp.zeros_like(co)
    p_copy.wait()

    def turn(i, carry):
        for t in range(3):
            pt[i, t * BLK:(t + 1) * BLK, :] = p_v[tbl[i, 25 + t]].T
        return carry

    lax.fori_loop(0, ROWS, turn, 0)

    def gathered(ref, i, first_col, stride, aa, cols):
        return jnp.concatenate(
            [jnp.concatenate([ref[tbl[i, first_col + a * stride + o]] for o in cols], axis=1) for a in range(aa)],
            axis=0)

    def local_rows(start, count, plan):
        def step(n, carry):
            i = start + n
            lhs = jnp.concatenate([a_v[i, a] for a in range(5)], axis=1)
            for cols, keep, base in plan:
                got = jnp.dot(lhs, gathered(p_v, i, 0, 5, 5, cols), preferred_element_type=F32)
                lo = (cols[0] - base) * BLK
                hi = (cols[-1] + 1 - base) * BLK
                if keep is None:
                    m_v[i, :, lo:hi] = got.astype(BF16)
                else:
                    keep[n, :, lo:hi] = got
            return carry

        lax.fori_loop(0, count, step, 0)

    a_copies[1].wait()
    a_copies[2].wait()
    local_rows(AGG, 2 * AGG, (((0, 1), None, 0), ((2, 3), None, 0), ((4,), None, 0)))
    a_copies[0].wait()
    local_rows(0, AGG, (((0, 1), acc_lo, 0), ((2,), acc_lo, 0), ((3, 4), None, 0)))
    a_copies[3].wait()
    local_rows(3 * AGG, AGG, (((0, 1), None, 0), ((2, 3), acc_hi, 2), ((4,), acc_hi, 2)))

    def lift(k):
        lhs = jnp.concatenate([pt[k * AGG + n] for n in range(AGG)], axis=1)
        for cols in ((0, 1), (2, 3), (4,)):
            rhs = m_v[k * AGG:(k + 1) * AGG, :, cols[0] * BLK:(cols[-1] + 1) * BLK]
            rhs = rhs.reshape(AGG * BLK, len(cols) * BLK)
            got = jnp.dot(lhs, rhs, preferred_element_type=F32)
            for t in range(3):
                for n, o in enumerate(cols):
                    co[k + t, o - t + 2] += got[t * BLK:(t + 1) * BLK, n * BLK:(n + 1) * BLK]

    lift(1)
    lift(2)

    def halo_rows(start, ref, keep, base):
        def step(n, carry):
            i = start + n
            lhs = jnp.concatenate([a_v[i, a] for a in range(1, 5)], axis=1)
            for cols in ((0, 1), (2,)):
                got = jnp.dot(lhs, gathered(ref, i, 28, 3, 4, cols), preferred_element_type=F32)
                lo = cols[0] * BLK
                hi = (cols[-1] + 1) * BLK
                m_v[i, :, base * BLK + lo:base * BLK + hi] = (keep[n, :, lo:hi] + got).astype(BF16)
            return carry

        lax.fori_loop(0, AGG, step, 0)

    def send_partial(side, row, first_s, target, slot):
        ps_s[side] = jnp.zeros_like(ps_s[side])
        for n in range(5):
            q, scale = quantised(co[row, first_s + n])
            pq_s[side, n] = q
            ps_s[side, n:n + 1, :] = scale
        blocks = to_neighbour(slot, pq_s.at[side], pq_r.at[side], target)
        scales = to_neighbour(slot + 1, ps_s.at[side], ps_r.at[side], target)
        blocks.start()
        scales.start()
        return blocks, scales

    p_next.wait_recv()
    halo_rows(0, h_lo, acc_lo, 0)
    lift(0)
    sent_prev = send_partial(0, 0, 2, prv, 4)
    p_prev.wait_recv()
    halo_rows(3 * AGG, h_hi, acc_hi, 2)
    lift(3)
    sent_next = send_partial(1, 5, 0, nxt, 6)

    def pack(k):
        sb[k] = jnp.zeros_like(sb[k])
        for s in range(7):
            q, scale = quantised(co[k + 1, s])
            qb[k, s] = q
            sb[k, s:s + 1, :] = scale

    qb[AGGS] = jnp.zeros_like(qb[AGGS])
    sb[AGGS] = jnp.zeros_like(sb[AGGS])
    pack(1)
    pack(2)
    for copy in sent_prev:
        copy.wait_recv()
    for n in range(5):
        co[4, 2 + n] += pq_r[0, n].astype(jnp.int32).astype(F32) * ps_r[0, n:n + 1, :]
    pack(3)
    for copy in sent_next:
        copy.wait_recv()
    for n in range(5):
        co[1, n] += pq_r[1, n].astype(jnp.int32).astype(F32) * ps_r[1, n:n + 1, :]
    pack(0)

    def to_owner(off, src, dst, send, recv):
        return pltpu.make_async_remote_copy(
            src_ref=src.at[off], dst_ref=dst.at[g], send_sem=send.at[off], recv_sem=recv.at[off],
            device_id=((g + off) % groups, r), device_id_type=MESH)

    def from_maker(off, src, dst, send, recv):
        return pltpu.make_async_remote_copy(
            src_ref=src.at[off], dst_ref=dst.at[(g + groups - off) % groups], send_sem=send.at[off],
            recv_sem=recv.at[off], device_id=((g + groups - off) % groups, r), device_id_type=MESH)

    order = (4, 3, 5, 2, 6, 1, 7)
    for off in order + (0,):
        k = sel[(g + off) % groups]
        sq[off] = qb[k]
        ss[off] = sb[k]
        if off:
            to_owner(off, sq, q_out, gq_send, gq_recv).start()
            to_owner(off, ss, sc_out, gs_send, gs_recv).start()
    own_q = pltpu.make_async_copy(sq.at[0], q_out.at[g], self_sem.at[0])
    own_s = pltpu.make_async_copy(ss.at[0], sc_out.at[g], self_sem.at[1])
    own_q.start()
    own_s.start()

    x_next.wait_recv()
    x_prev.wait_recv()

    def applied(k, mine, halo, scale_by):
        total = None
        for s in range(7):
            c = k + s - 3
            if c < 0:
                row = halo[0, AGGS + c:AGGS + c + 1, :]
            elif c < AGGS:
                row = mine[c:c + 1, :]
            else:
                row = halo[1, c - AGGS:c - AGGS + 1, :]
            if scale_by is not None:
                row = row / scale_by
            term = co[k + 1, s] * row
            total = term if total is None else total + term
        return jnp.sum(total.T, axis=0, keepdims=True)

    center, old_weight, resid_weight = par[0], par[1], par[2]
    own2[...] = jnp.zeros_like(own2)
    for k in range(AGGS):
        rhs = own[k:k + 1, :]
        x1 = rhs / center
        own2[k:k + 1, :] = x1 + old_weight * x1 + resid_weight * (rhs - applied(k, own, halo_x, center))
    x2_next = to_neighbour(8, own2, halo_x2.at[0], nxt)
    x2_prev = to_neighbour(9, own2, halo_x2.at[1], prv)
    x2_next.start()
    x2_prev.start()
    xrb[...] = jnp.zeros_like(xrb)
    x2_next.wait_recv()
    x2_prev.wait_recv()
    for k in range(AGGS):
        xrb[k, 0:1, :] = own2[k:k + 1, :]
        xrb[k, 1:2, :] = own[k:k + 1, :] - applied(k, own2, halo_x2, None)
    for off in order + (0,):
        sx[off] = xrb[sel[(g + off) % groups]]
        if off:
            to_owner(off, sx, xr_out, gx_send, gx_recv).start()
    own_x = pltpu.make_async_copy(sx.at[0], xr_out.at[g], self_sem.at[2])
    own_x.start()

    for copy in (p_next, p_prev, x_next, x_prev, *sent_prev, *sent_next, x2_next, x2_prev):
        copy.wait_send()
    for off in order:
        for args in ((sq, q_out, gq_send, gq_recv), (ss, sc_out, gs_send, gs_recv), (sx, xr_out, gx_send, gx_recv)):
            to_owner(off, *args).wait_send()
            from_maker(off, *args).wait_recv()
    own_q.wait()
    own_s.wait()
    own_x.wait()


def call_kernel(groups, rows_axis, tbl, sel, par, a, p, rhs):
    hbm = pl.BlockSpec(memory_space=pl.ANY)
    smem = pl.BlockSpec(memory_space=pltpu.SMEM)
    vmem = pl.BlockSpec(memory_space=pltpu.VMEM)
    dma = pltpu.SemaphoreType.DMA
    i16 = jnp.int16
    return pl.pallas_call(
        functools.partial(kernel, groups, rows_axis),
        out_shape=(
            jax.ShapeDtypeStruct((groups, 7, BLK, BLK), i16),
            jax.ShapeDtypeStruct((groups, 8, BLK), F32),
            jax.ShapeDtypeStruct((groups, 8, BLK), F32),
        ),
        in_specs=[smem, smem, smem, hbm, hbm, vmem],
        out_specs=(hbm, hbm, hbm),
        scratch_shapes=[
            pltpu.VMEM((ROWS, 5, BLK, BLK), BF16),
            pltpu.VMEM((2 * ROWS + 1, BLK, BLK), BF16),
            pltpu.VMEM((2 * AGG + 1, BLK, BLK), BF16),
            pltpu.VMEM((2 * AGG + 1, BLK, BLK), BF16),
            pltpu.VMEM((ROWS, 3 * BLK, BLK), BF16),
            pltpu.VMEM((ROWS, BLK, 5 * BLK), BF16),
            pltpu.VMEM((AGG, BLK, 3 * BLK), F32),
            pltpu.VMEM((AGG, BLK, 3 * BLK), F32),
            pltpu.VMEM((AGGS + 2, 7, BLK, BLK), F32),
            pltpu.VMEM((AGGS + 1, 7, BLK, BLK), i16),
            pltpu.VMEM((AGGS + 1, 8, BLK), F32),
            pltpu.VMEM((groups, 7, BLK, BLK), i16),
            pltpu.VMEM((groups, 8, BLK), F32),
            pltpu.VMEM((AGGS + 1, 8, BLK), F32),
            pltpu.VMEM((groups, 8, BLK), F32),
            pltpu.VMEM((2, 5, BLK, BLK), i16),
            pltpu.VMEM((2, 8, BLK), F32),
            pltpu.VMEM((2, 5, BLK, BLK), i16),
            pltpu.VMEM((2, 8, BLK), F32),
            pltpu.VMEM((8, BLK), F32),
            pltpu.VMEM((2, 8, BLK), F32),
            pltpu.VMEM((8, BLK), F32),
            pltpu.VMEM((2, 8, BLK), F32),
            dma((AGGS,)), dma, dma((10,)), dma((10,)),
            dma((groups,)), dma((groups,)), dma((groups,)), dma((groups,)), dma((groups,)), dma((groups,)),
            dma((3,)),
        ],
        compiler_params=pltpu.CompilerParams(
            collective_id=0, has_side_effects=True, vmem_limit_bytes=56 << 20),
    )(tbl, sel, par, a, p, rhs)


def tables(fine_cols, prolong_cols, agg_owner, device, devices, groups):
    fine_total = ROWS * devices
    coarse_total = AGGS * devices
    first_row = device * ROWS
    base = device * AGGS
    pieces = [
        lax.dynamic_slice_in_dim(prolong_cols, (first_row - AGG) % fine_total, AGG, 0),
        lax.dynamic_slice_in_dim(prolong_cols, first_row, ROWS, 0),
        lax.dynamic_slice_in_dim(prolong_cols, (first_row + ROWS) % fine_total, AGG, 0),
    ]
    cols_pad = (jnp.concatenate(pieces, axis=0) - base + 8) % coarse_total - 8
    local = jnp.arange(ROWS, dtype=jnp.int32)
    reach = (fine_cols - (first_row + local)[:, None] + AGG) % fine_total - AGG
    where = local[:, None] + AGG + reach
    hit = where[:, :, None] == jnp.arange(ROWS + 2 * AGG, dtype=jnp.int32)
    near = jnp.sum(jnp.where(hit[..., None], cols_pad[None, None], 0), axis=2)
    offset = near - (local // AGG)[:, None, None] + 2
    match = offset[:, :, None, :] == jnp.arange(5, dtype=jnp.int32)[:, None]
    block = 2 * where[:, :, None] + jnp.arange(2, dtype=jnp.int32)
    inside = (where >= AGG) & (where < ROWS + AGG)

    def table(ok, shift, none):
        picked = jnp.where(match & ok[:, :, None, None], block[:, :, None, :] - shift - none, 0)
        return jnp.sum(picked, axis=3) + none

    here = table(inside, 2 * AGG, 2 * ROWS)
    below = table(where < AGG, 0, 2 * AGG)[:, 1:, 0:3]
    above = table(where >= ROWS + AGG, 2 * (ROWS + AGG), 2 * AGG)[:, 1:, 2:5]
    halo = jnp.where((local < 2 * AGG)[:, None, None], below, above)
    own = cols_pad[AGG:ROWS + AGG] - (local // AGG)[:, None] + 1
    own_match = own[:, None, :] == jnp.arange(3, dtype=jnp.int32)[:, None]
    own_block = (2 * local)[:, None] + jnp.arange(2, dtype=jnp.int32)
    mine = jnp.sum(jnp.where(own_match, own_block[:, None, :] - 2 * ROWS, 0), axis=2) + 2 * ROWS
    tbl = jnp.concatenate([here.reshape(ROWS, 25), mine, halo.reshape(ROWS, 12)], axis=1)
    owners = lax.dynamic_slice_in_dim(agg_owner, base, AGGS, 0)
    ids = jnp.arange(AGGS, dtype=jnp.int32)
    owned = owners[:, None] == jnp.arange(groups, dtype=jnp.int32)
    sel = jnp.sum(jnp.where(owned, (ids - AGGS)[:, None], 0), axis=0) + AGGS
    return tbl, sel


def per_device(
    fine_cols, fine_blocks, prolong_cols, prolong_blocks, agg_owner, coarse_rhs, lam_low, lam_high
):
    groups = lax.axis_size("grp")
    rows_axis = lax.axis_size("row")
    device = lax.axis_index("grp") * rows_axis + lax.axis_index("row")
    tbl, sel = tables(fine_cols, prolong_cols, agg_owner, device, groups * rows_axis, groups)
    par = jnp.stack(chebyshev_terms(lam_low, lam_high))
    q, scale, xr = call_kernel(
        groups, rows_axis, tbl, sel, par, fine_blocks, prolong_blocks.reshape(2 * ROWS, BLK, BLK), coarse_rhs)
    operator = q.astype(F32) * scale[:, :7, None, :]
    return operator, xr[:, 0], xr[:, 1]


def solution(mesh):
    return jax.shard_map(
        per_device,
        mesh=mesh,
        in_specs=(
            P(("grp", "row"), None),
            P(("grp", "row"), None, None, None),
            P(),
            P(("grp", "row"), None, None, None),
            P(),
            P(("grp", "row"), None),
            P(),
            P(),
        ),
        out_specs=(
            P(("grp", "row"), None, None, None),
            P(("grp", "row"), None),
            P(("grp", "row"), None),
        ),
        check_vma=False,
    )
```

time: 587 us -> 80.8 us (0.14)
  waiting for transfers between devices: 230 us -> 0 us
  local copies, waits for them, and re-layouts: 156 us -> 4.05 us
  matrix products: 143 us -> 0 us
  Pallas kernels: 0 us -> 66.7 us
  starting transfers between devices: 25.5 us -> 0 us
  between operations: 15.7 us -> 2.21 us
  loops' own time: 5.94 us -> 0 us
    all_gather x2 -> x0, waiting for transfers between devices: 202 us -> none  [operate(): whole = lax.all_gather(vector, ('grp', 'row'), axis=0, tiled=True)]
    dot_general x20 -> x0, matrix products: 143 us -> none  [the longest x4 49.6 us: one_aggregate(): return jnp.einsum('ipots,ipokn->tskn', placing, term_blocks, precision=HIGH)]
    transpose x8 -> x0, local copies, waits for them, and re-layouts: 86.4 us -> none  [the longest x4 45.9 us: one_aggregate(): jnp.einsum('ipmk,iomn->ipokn', own_blocks, merged, preferred_element_type...]
    pallas_call x0 -> x1, Pallas kernels: none -> 66.7 us  [call_kernel(): pl.pallas_call(functools.partial(kernel, groups, rows_axis), out_shape=(j...]
    gather x29 -> x0, local copies, waits for them, and re-layouts: 47.9 us -> none  [the longest x8 36.6 us: one_aggregate(): p_near = jnp.take(p_pad, positions, axis=0)]
    ppermute x4 -> x0, waiting for transfers between devices: 27.5 us -> none  [the longest x2 25.1 us: extended_2(): lax.ppermute(lax.slice_in_dim(block, block.shape[dim] - width, None, axis...]
    all_to_all x2 -> x0, starting transfers between devices: 15.9 us -> none  [the longest x1 9.09 us: per_device(): lax.all_to_all(send_rows, 'grp', split_axis=0, concat_axis=0, tiled=True)]
    unnamed x13 -> x0, local copies, waits for them, and re-layouts: 9.64 us -> none
  transfers between devices with their start and end apart: 8 -> 0, of which waited for: 5 -> 0; matrix products, arithmetic and copies ran while one was open for 3% -> 0% of each run, Pallas kernels for 0% -> 0%
where the time goes in v1:
time: 80.8 us; the launch traced here: 80.4 us
  Pallas kernels  66.7 us (83%)
  other arithmetic  7.42 us (9%)
  local copies, waits for them, and re-layouts  4.05 us (5%)
  between operations  2.21 us (3%)
    pallas_call x1, Pallas kernels, call_kernel(): pl.pallas_call(functools.partial(kernel, groups, rows_axis), out_shape=(j...  66.7 us
    mul x1, other arithmetic, per_device(): operator = q.astype(F32) * scale[:, :7, None, :]  4.02 us

profile of v1, /device:TPU:1, one launch (start us, length us, event | category | flops | bytes accessed | tf_op | source)
XLA Modules:
  0.0 80.4 jit_solution(7620814684718786836)
XLA Ops:
  2.1 0.7 pad_maximum_fusion.par
  2.8 0.8 dynamic_slice.15
  3.6 0.8 constant_dynamic-slice_fusion.1
  4.3 0.1 select_reduce_fusion.1
  4.4 0.5 broadcast_add_fusion.2.sel
  4.9 0.8 %constant_dynamic-slice_fusion.2 = (s32[10,2]{0,1:T(2,128)S(1)}, s32[10,2]{0,1:T(2,128)S(1)}) fusion(s32[10240,2]{0,1:T(2,128)} %param.10, s32[]{:T(128)S(6)} %select_n.83, s32[]{:T(128)S(6)} %select_n.86), kind=kLoop, calls=%fused_computation.48 | loop fusion | bytes 328 | tf_op jit(solution)/shard_map/dynamic_slice | solution.py:326
  5.8 0.1 fusion.10
  5.8 0.1 add_add_fusion
  6.0 0.7 broadcast_compare_fusion.1
  6.7 0.1 copy.30
  6.8 0.1 iota_compare_fusion
  6.9 0.3 select_reduce_fusion
  7.2 0.1 fusion
  7.3 0.1 copy.32
  7.4 0.1 copy.33
  7.5 0.7 pad_add_fusion.tbl
  8.2 66.7 %shard_map.103 = (s16[8,7,128,128]{3,2,1,0:T(8,128)(2,1)}, f32[8,8,128]{2,1,0:T(8,128)}, f32[8,8,128]{2,1,0:T(8,128)}) custom-call(s32[40,40]{1,0:T(8,128)} %pad_add_fusion.tbl, s32[8]{0:T(128)} %broadcast_add_fusion.2.sel, f32[3]{0:T(128)} %pad_maximum_fusion.par, bf16[40,5,128,128]{3,2,1,0:T(8,128)(2,1)} %a_hbm.1, bf16[80,128,128]{2,1,0:T(8,128)(2,1)} %bitcast.12, ...), custom_call_target="tpu_custom_call" | custom-call | tf_op jit(solution)/shard_map/pallas_call | solution.py:278
  75.0 1.4 %fusion.14 = (f32[8,1,128]{2,1,0:T(1,128)}, f32[8,1,128]{2,1,0:T(1,128)}) fusion(f32[8,8,128]{2,1,0:T(8,128)} %get-tuple-element.8), kind=kLoop, calls=%fused_computation.56 | loop fusion | bytes 16384 | tf_op jit(solution)/shard_map/slice | solution.py:372
  76.4 4.0 %convert_multiply_fusion = f32[8,7,128,128]{3,2,1,0:T(8,128)} fusion(s16[8,7,128,128]{3,2,1,0:T(8,128)(2,1)} %get-tuple-element.6, f32[8,7,128]{2,1,0:T(8,128)} %bitcast.13), kind=kLoop, calls=%fused_computation | loop fusion | flops 1835008 | bytes 5533696 | tf_op jit(solution)/shard_map/mul | solution.py:371
  (15 shorter events, 0.1 us)

commit v2 on v1

v2 whole, which is shorter than its diff:
```python
import functools

import jax
import jax.numpy as jnp
from jax import lax
from jax.experimental import pallas as pl
from jax.experimental.pallas import tpu as pltpu
from jax.sharding import PartitionSpec as P

MESH = pl.DeviceIdType.MESH
BLK = 128
AGG = 10
AGGS = 4
ROWS = AGG * AGGS
F32 = jnp.float32
BF16 = jnp.bfloat16
Q_MAX = 32767.0
TINY = 2.0**-110
SHIFT = (5, 3, 0, 0)
EARLY = 2


def quantised(block):
    top = jnp.maximum(jnp.max(jnp.abs(block), axis=0, keepdims=True), TINY)
    q = jnp.floor(block * (Q_MAX / top) + 0.5).astype(jnp.int32).astype(jnp.int16)
    return q, top * (1.0 / Q_MAX)


def chebyshev_terms(low, high):
    center = 0.5 * (high + low)
    radius = 0.5 * (high - low)
    sigma_ratio = center / radius
    first_rho = 1.0 / sigma_ratio
    second_rho = 1.0 / (2.0 * sigma_ratio - first_rho)
    return center, second_rho * first_rho, 2.0 * second_rho / radius


def wrapped(x, total):
    x = jnp.where(x > total // 2, x - total, x)
    return jnp.where(x < -(total // 2), x + total, x)


def write_tables(fine_total, coarse_total, first_row, base, fc, pc, tbl):
    row = lax.broadcasted_iota(jnp.int32, (5, ROWS), 1)
    reach = wrapped(fc[...] - (first_row + row), fine_total)
    place = row + AGG + reach
    near = [jnp.zeros((5, ROWS), jnp.int32) for _ in range(2)]
    start = (first_row + fine_total - AGG) % fine_total
    for p in range(ROWS + 2 * AGG):
        at = (start + p) % fine_total
        for q in range(2):
            near[q] = jnp.where(place == p, pc[q, at], near[q])
    agg = jnp.zeros((5, ROWS), jnp.int32)
    for k in range(1, AGGS):
        agg = agg + jnp.where(row >= k * AGG, 1, 0)
    offset = [wrapped(c - base - agg, coarse_total) + 2 for c in near]

    def pick(o, ok, block, none):
        got = jnp.where(ok & (offset[0] == o), block, none)
        return jnp.where(ok & (offset[1] == o), block + 1, got)

    inside = (place >= AGG) & (place < ROWS + AGG)
    for o in range(5):
        tbl[o, 0:5, 0:ROWS] = pick(o, inside, 2 * (place - AGG), 2 * ROWS)
    for o in range(3):
        below = pick(o, (place >= 0) & (place < AGG), 2 * place, 2 * AGG)
        above = pick(
            o + 2, (place >= ROWS + AGG) & (place < ROWS + 2 * AGG), 2 * (place - ROWS - AGG), 2 * AGG)
        tbl[5 + o, 0:5, 0:ROWS] = jnp.where(row < 2 * AGG, below, above)
    everywhere = row >= 0
    for t in range(3):
        tbl[8 + t, 0:5, 0:ROWS] = pick(t + 1, everywhere, 2 * row, 2 * ROWS)


def kernel(
    groups, rows_axis,
    pc, owner, lam_low, lam_high, fc, a_hbm, p_hbm, rhs_ref,
    q_out, sc_out, xr_out,
    tbl_v, tbl, a_v, p_v, h_lo, h_hi, pt, m_v, acc_lo, acc_hi, co, qb, sb, sq, ss, xrb, sx,
    pq_s, ps_s, pq_r, ps_r, own, halo_x, own2, halo_x2,
    a_sem, p_sem, t_sem, nb_send, nb_recv, ge_send, ge_recv, gq_send, gq_recv, gs_send, gs_recv, gx_send, gx_recv,
    self_sem,
):
    g = lax.axis_index("grp")
    r = lax.axis_index("row")
    device = g * rows_axis + r
    devices = groups * rows_axis
    base = device * AGGS
    last = (r + 1) // rows_axis
    nxt = ((g + last) % groups, (r + 1) % rows_axis)
    first = (rows_axis - r) // rows_axis
    prv = ((g + groups - first) % groups, (r + rows_axis - 1) % rows_axis)

    barrier = pltpu.get_barrier_semaphore()
    for target in (nxt, prv):
        pl.semaphore_signal(barrier, inc=1, device_id=target, device_id_type=MESH)
    for off in range(1, groups):
        pl.semaphore_signal(barrier, inc=1, device_id=((g + off) % groups, r), device_id_type=MESH)

    p_copy = pltpu.make_async_copy(p_hbm, p_v.at[pl.ds(0, 2 * ROWS)], p_sem)
    p_copy.start()
    a_copies = [
        pltpu.make_async_copy(a_hbm.at[pl.ds(k * AGG, AGG)], a_v.at[pl.ds(k * AGG, AGG)], a_sem.at[k])
        for k in range(AGGS)
    ]
    for k in (0, 1, 2, 3):
        a_copies[k].start()

    own[...] = jnp.zeros_like(own)
    own[0:AGGS, :] = rhs_ref[...]
    tbl_v[...] = jnp.zeros_like(tbl_v)
    write_tables(ROWS * devices, AGGS * devices, device * ROWS, base, fc, pc, tbl_v)
    t_copy = pltpu.make_async_copy(tbl_v, tbl, t_sem)
    t_copy.start()

    pl.semaphore_wait(barrier, groups + 1)

    def to_neighbour(slot, src, dst, target):
        return pltpu.make_async_remote_copy(
            src_ref=src, dst_ref=dst, send_sem=nb_send.at[slot], recv_sem=nb_recv.at[slot],
            device_id=target, device_id_type=MESH)

    p_next = to_neighbour(0, p_hbm.at[pl.ds(2 * (ROWS - AGG), 2 * AGG)], h_lo.at[pl.ds(0, 2 * AGG)], nxt)
    p_prev = to_neighbour(1, p_hbm.at[pl.ds(0, 2 * AGG)], h_hi.at[pl.ds(0, 2 * AGG)], prv)
    p_next.start()
    p_prev.start()
    x_next = to_neighbour(2, own, halo_x.at[0], nxt)
    x_prev = to_neighbour(3, own, halo_x.at[1], prv)
    x_next.start()
    x_prev.start()

    zero_block = jnp.zeros((BLK, BLK), BF16)
    p_v[2 * ROWS] = zero_block
    h_lo[2 * AGG] = zero_block
    h_hi[2 * AGG] = zero_block
    co[...] = jnp.zeros_like(co)
    t_copy.wait()
    p_copy.wait()

    def turn(i, carry):
        for t in range(3):
            pt[i, t * BLK:(t + 1) * BLK, :] = p_v[tbl[8 + t, 0, i]].T
        return carry

    lax.fori_loop(0, ROWS, turn, 0)

    def gathered(ref, i, plane, entries, cols):
        return jnp.concatenate(
            [jnp.concatenate([ref[tbl[plane + o, a, i]] for o in cols], axis=1) for a in entries], axis=0)

    def local_rows(start, count, plan):
        def step(n, carry):
            i = start + n
            lhs = jnp.concatenate([a_v[i, a] for a in range(5)], axis=1)
            for cols, keep, first_col in plan:
                got = jnp.dot(lhs, gathered(p_v, i, 0, range(5), cols), preferred_element_type=F32)
                lo = (cols[0] - first_col) * BLK
                hi = (cols[-1] + 1 - first_col) * BLK
                if keep is None:
                    m_v[i, :, lo:hi] = got.astype(BF16)
                else:
                    keep[n, :, lo:hi] = got
            return carry

        lax.fori_loop(0, count, step, 0)

    def lift(k, groups_of_cols):
        lhs = jnp.concatenate([pt[k * AGG + n] for n in range(AGG)], axis=1)
        for cols in groups_of_cols:
            rhs = m_v[k * AGG:(k + 1) * AGG, :, cols[0] * BLK:(cols[-1] + 1) * BLK]
            rhs = rhs.reshape(AGG * BLK, len(cols) * BLK)
            got = jnp.dot(lhs, rhs, preferred_element_type=F32)
            for t in range(3):
                for n, o in enumerate(cols):
                    co[k + t, o - t + 2] += got[t * BLK:(t + 1) * BLK, n * BLK:(n + 1) * BLK]

    a_copies[0].wait()
    local_rows(0, AGG, (((0, 1), acc_lo, 0), ((2,), acc_lo, 0), ((3, 4), None, 0)))
    lift(0, ((3, 4),))
    a_copies[1].wait()
    a_copies[2].wait()
    local_rows(AGG, 2 * AGG, (((0, 1), None, 0), ((2, 3), None, 0), ((4,), None, 0)))
    lift(1, ((0, 1), (2, 3), (4,)))
    lift(2, ((0, 1), (2, 3), (4,)))
    a_copies[3].wait()
    local_rows(3 * AGG, AGG, (((0, 1), None, 0), ((2, 3), acc_hi, 2), ((4,), acc_hi, 2)))
    lift(3, ((0, 1),))

    def pack(k, places):
        for place in places:
            s = (place + SHIFT[k]) % 7
            q, scale = quantised(co[k + 1, s])
            qb[k, place] = q
            sb[k, place:place + 1, :] = scale

    def owned(dest):
        k = AGGS
        for c in range(AGGS):
            k = jnp.where(owner[base + c] == dest, c, k)
        return k

    def to_owner(off, src, dst, send, recv, lo, hi):
        return pltpu.make_async_remote_copy(
            src_ref=src.at[off, pl.ds(lo, hi - lo)], dst_ref=dst.at[g, pl.ds(lo, hi - lo)],
            send_sem=send.at[off], recv_sem=recv.at[off],
            device_id=((g + off) % groups, r), device_id_type=MESH)

    def from_maker(off, src, dst, send, recv, lo, hi):
        return pltpu.make_async_remote_copy(
            src_ref=src.at[off, pl.ds(lo, hi - lo)],
            dst_ref=dst.at[(g + groups - off) % groups, pl.ds(lo, hi - lo)], send_sem=send.at[off],
            recv_sem=recv.at[off], device_id=((g + groups - off) % groups, r), device_id_type=MESH)

    order = (4, 3, 5, 2, 6, 1, 7)
    early = (sq, q_out, ge_send, ge_recv, 0, EARLY)
    late = (sq, q_out, gq_send, gq_recv, EARLY, 7)
    scales = (ss, sc_out, gs_send, gs_recv, 0, 8)
    vectors = (sx, xr_out, gx_send, gx_recv, 0, 8)
    qb[AGGS] = jnp.zeros_like(qb[AGGS])
    sb[...] = jnp.zeros_like(sb)
    for k in range(AGGS):
        pack(k, range(EARLY))
    for off in order + (0,):
        sq[off, 0:EARLY] = qb[owned((g + off) % groups), 0:EARLY]
        if off:
            to_owner(off, *early).start()

    def halo_rows(start, ref, keep, first_col):
        def step(n, carry):
            i = start + n
            lhs = jnp.concatenate([a_v[i, a] for a in range(1, 5)], axis=1)
            for cols in ((0, 1), (2,)):
                got = jnp.dot(lhs, gathered(ref, i, 5, range(1, 5), cols), preferred_element_type=F32)
                lo = cols[0] * BLK
                hi = (cols[-1] + 1) * BLK
                m_v[i, :, first_col * BLK + lo:first_col * BLK + hi] = (keep[n, :, lo:hi] + got).astype(BF16)
            return carry

        lax.fori_loop(0, AGG, step, 0)

    def send_partial(part, side, row, all_s, target, slot):
        lo, hi = ((0, 2), (2, 5))[part]
        ps_s[side, part] = jnp.zeros_like(ps_s[side, part])
        for n in range(lo, hi):
            q, scale = quantised(co[row, all_s[n]])
            pq_s[side, n] = q
            ps_s[side, part, n:n + 1, :] = scale
        copies = (
            to_neighbour(slot, pq_s.at[side, pl.ds(lo, hi - lo)], pq_r.at[side, pl.ds(lo, hi - lo)], target),
            to_neighbour(slot + 1, ps_s.at[side, part], ps_r.at[side, part], target),
        )
        for copy in copies:
            copy.start()
        return copies

    down = (5, 6, 2, 3, 4)
    up = (0, 1, 2, 3, 4)
    p_next.wait_recv()
    sent_down = send_partial(0, 0, 0, down, prv, 4)
    halo_rows(0, h_lo, acc_lo, 0)
    lift(0, ((0, 1), (2,)))
    sent_down += send_partial(1, 0, 0, down, prv, 6)
    p_prev.wait_recv()
    sent_up = send_partial(0, 1, 5, up, nxt, 8)
    halo_rows(3 * AGG, h_hi, acc_hi, 2)
    lift(3, ((2, 3), (4,)))
    sent_up += send_partial(1, 1, 5, up, nxt, 10)
    pack(1, range(EARLY, 7))
    pack(2, range(EARLY, 7))

    def receive_partial(copies, side, row, all_s):
        for copy in copies:
            copy.wait_recv()
        for n in range(5):
            part = 0 if n < 2 else 1
            co[row, all_s[n]] += pq_r[side, n].astype(jnp.int32).astype(F32) * ps_r[side, part, n:n + 1, :]

    receive_partial(sent_down, 0, AGGS, down)
    pack(3, range(EARLY, 7))
    receive_partial(sent_up, 1, 1, up)
    pack(0, range(EARLY, 7))
    for off in order + (0,):
        k = owned((g + off) % groups)
        sq[off, EARLY:7] = qb[k, EARLY:7]
        ss[off] = sb[k]
        if off:
            to_owner(off, *late).start()
            to_owner(off, *scales).start()
    own_q = pltpu.make_async_copy(sq.at[0], q_out.at[g], self_sem.at[0])
    own_s = pltpu.make_async_copy(ss.at[0], sc_out.at[g], self_sem.at[1])
    own_q.start()
    own_s.start()

    x_next.wait_recv()
    x_prev.wait_recv()
    center, old_weight, resid_weight = chebyshev_terms(
        jnp.full((1, BLK), lam_low[0], F32), jnp.full((1, BLK), lam_high[0], F32))

    def applied(k, mine, halo, scale_by):
        total = None
        for s in range(7):
            c = k + s - 3
            if c < 0:
                row = halo[0, AGGS + c:AGGS + c + 1, :]
            elif c < AGGS:
                row = mine[c:c + 1, :]
            else:
                row = halo[1, c - AGGS:c - AGGS + 1, :]
            if scale_by is not None:
                row = row / scale_by
            term = co[k + 1, s] * row
            total = term if total is None else total + term
        return jnp.sum(total.T, axis=0, keepdims=True)

    own2[...] = jnp.zeros_like(own2)
    for k in range(AGGS):
        rhs = own[k:k + 1, :]
        x1 = rhs / center
        own2[k:k + 1, :] = x1 + old_weight * x1 + resid_weight * (rhs - applied(k, own, halo_x, center))
    x2_next = to_neighbour(12, own2, halo_x2.at[0], nxt)
    x2_prev = to_neighbour(13, own2, halo_x2.at[1], prv)
    x2_next.start()
    x2_prev.start()
    xrb[...] = jnp.zeros_like(xrb)
    x2_next.wait_recv()
    x2_prev.wait_recv()
    for k in range(AGGS):
        xrb[k, 0:1, :] = own2[k:k + 1, :]
        xrb[k, 1:2, :] = own[k:k + 1, :] - applied(k, own2, halo_x2, None)
    for off in order + (0,):
        sx[off] = xrb[owned((g + off) % groups)]
        if off:
            to_owner(off, *vectors).start()
    own_x = pltpu.make_async_copy(sx.at[0], xr_out.at[g], self_sem.at[2])
    own_x.start()

    for copy in (p_next, p_prev, x_next, x_prev, *sent_down, *sent_up, x2_next, x2_prev):
        copy.wait_send()
    for off in order:
        for args in (early, late, scales, vectors):
            to_owner(off, *args).wait_send()
            from_maker(off, *args).wait_recv()
    own_q.wait()
    own_s.wait()
    own_x.wait()


def call_kernel(groups, rows_axis, pc, owner, lam_low, lam_high, fc, a, p, rhs):
    hbm = pl.BlockSpec(memory_space=pl.ANY)
    smem = pl.BlockSpec(memory_space=pltpu.SMEM)
    vmem = pl.BlockSpec(memory_space=pltpu.VMEM)
    dma = pltpu.SemaphoreType.DMA
    i16 = jnp.int16
    return pl.pallas_call(
        functools.partial(kernel, groups, rows_axis),
        out_shape=(
            jax.ShapeDtypeStruct((groups, 7, BLK, BLK), i16),
            jax.ShapeDtypeStruct((groups, 8, BLK), F32),
            jax.ShapeDtypeStruct((groups, 8, BLK), F32),
        ),
        in_specs=[smem, smem, smem, smem, vmem, hbm, hbm, vmem],
        out_specs=(hbm, hbm, hbm),
        scratch_shapes=[
            pltpu.VMEM((11, 8, BLK), jnp.int32),
            pltpu.SMEM((11, 8, BLK), jnp.int32),
            pltpu.VMEM((ROWS, 5, BLK, BLK), BF16),
            pltpu.VMEM((2 * ROWS + 1, BLK, BLK), BF16),
            pltpu.VMEM((2 * AGG + 1, BLK, BLK), BF16),
            pltpu.VMEM((2 * AGG + 1, BLK, BLK), BF16),
            pltpu.VMEM((ROWS, 3 * BLK, BLK), BF16),
            pltpu.VMEM((ROWS, BLK, 5 * BLK), BF16),
            pltpu.VMEM((AGG, BLK, 3 * BLK), F32),
            pltpu.VMEM((AGG, BLK, 3 * BLK), F32),
            pltpu.VMEM((AGGS + 2, 7, BLK, BLK), F32),
            pltpu.VMEM((AGGS + 1, 7, BLK, BLK), i16),
            pltpu.VMEM((AGGS + 1, 8, BLK), F32),
            pltpu.VMEM((groups, 7, BLK, BLK), i16),
            pltpu.VMEM((groups, 8, BLK), F32),
            pltpu.VMEM((AGGS + 1, 8, BLK), F32),
            pltpu.VMEM((groups, 8, BLK), F32),
            pltpu.VMEM((2, 5, BLK, BLK), i16),
            pltpu.VMEM((2, 2, 8, BLK), F32),
            pltpu.VMEM((2, 5, BLK, BLK), i16),
            pltpu.VMEM((2, 2, 8, BLK), F32),
            pltpu.VMEM((8, BLK), F32),
            pltpu.VMEM((2, 8, BLK), F32),
            pltpu.VMEM((8, BLK), F32),
            pltpu.VMEM((2, 8, BLK), F32),
            dma((AGGS,)), dma, dma, dma((14,)), dma((14,)),
            dma((groups,)), dma((groups,)), dma((groups,)), dma((groups,)),
            dma((groups,)), dma((groups,)), dma((groups,)), dma((groups,)),
            dma((3,)),
        ],
        compiler_params=pltpu.CompilerParams(
            collective_id=0, has_side_effects=True, vmem_limit_bytes=56 << 20),
    )(pc, owner, lam_low, lam_high, fc, a, p, rhs)


def open_slots(rows_axis, owner, q_ref, scale_ref, xr_ref, out_ref, x_ref, r_ref):
    slot = pl.program_id(0)
    g = lax.axis_index("grp")
    maker = slot * rows_axis + lax.axis_index("row")
    shift = 0
    for k in range(AGGS):
        shift = jnp.where(owner[maker * AGGS + k] == g, SHIFT[k], shift)
    for s in range(7):
        place = s - shift
        place = jnp.where(place < 0, place + 7, place)
        out_ref[0, s] = q_ref[0, place].astype(jnp.int32).astype(F32) * scale_ref[0, pl.ds(place, 1), :]

    @pl.when(slot == 0)
    def _():
        for n in range(x_ref.shape[0]):
            x_ref[n:n + 1, :] = xr_ref[n, 0:1, :]
            r_ref[n:n + 1, :] = xr_ref[n, 1:2, :]


def call_open(groups, rows_axis, owner, q, scale, xr):
    whole = pl.BlockSpec((groups, BLK), lambda n, owner: (0, 0))
    return pl.pallas_call(
        functools.partial(open_slots, rows_axis),
        out_shape=(
            jax.ShapeDtypeStruct((groups, 7, BLK, BLK), F32),
            jax.ShapeDtypeStruct((groups, BLK), F32),
            jax.ShapeDtypeStruct((groups, BLK), F32),
        ),
        grid_spec=pltpu.PrefetchScalarGridSpec(
            num_scalar_prefetch=1,
            grid=(groups,),
            in_specs=[
                pl.BlockSpec((1, 7, BLK, BLK), lambda n, owner: (n, 0, 0, 0)),
                pl.BlockSpec((1, 8, BLK), lambda n, owner: (n, 0, 0)),
                pl.BlockSpec((groups, 8, BLK), lambda n, owner: (0, 0, 0)),
            ],
            out_specs=(
                pl.BlockSpec((1, 7, BLK, BLK), lambda n, owner: (n, 0, 0, 0)),
                whole,
                whole,
            ),
        ),
    )(owner, q, scale, xr)


def per_device(
    fine_cols, fine_blocks, prolong_cols, prolong_blocks, agg_owner, coarse_rhs, lam_low, lam_high
):
    groups = lax.axis_size("grp")
    rows_axis = lax.axis_size("row")
    q, scale, xr = call_kernel(
        groups, rows_axis, prolong_cols.T, agg_owner, lam_low, lam_high, fine_cols.T, fine_blocks,
        prolong_blocks.reshape(2 * ROWS, BLK, BLK), coarse_rhs)
    return call_open(groups, rows_axis, agg_owner, q, scale, xr)


def solution(mesh):
    return jax.shard_map(
        per_device,
        mesh=mesh,
        in_specs=(
            P(("grp", "row"), None),
            P(("grp", "row"), None, None, None),
            P(),
            P(("grp", "row"), None, None, None),
            P(),
            P(("grp", "row"), None),
            P(),
            P(),
        ),
        out_specs=(
            P(("grp", "row"), None, None, None),
            P(("grp", "row"), None),
            P(("grp", "row"), None),
        ),
        check_vma=False,
    )
```

time: 80.8 us -> 71.4 us (0.88)
  other arithmetic: 7.42 us -> 0 us
  local copies, waits for them, and re-layouts: 4.05 us -> 0 us
  Pallas kernels: 66.7 us -> 69.2 us
    pallas_call x0 -> x1, Pallas kernels: none -> 6.78 us  [call_open(): pl.pallas_call(functools.partial(open_slots, rows_axis), out_shape=(jax.S...]
    pallas_call x1, Pallas kernels: 66.7 us -> 62.4 us  [call_kernel(): pl.pallas_call(functools.partial(kernel, groups, rows_axis), out_shape=(j...]
    mul x3 -> x0, other arithmetic: 4.03 us -> none  [the longest x1 4.02 us: per_device(): operator = q.astype(F32) * scale[:, :7, None, :]]
    dynamic_slice x3 -> x0, local copies, waits for them, and re-layouts: 2.34 us -> none  [the longest x1 0.83 us: tables(): lax.dynamic_slice_in_dim(prolong_cols, (first_row - AGG) % fine_total, AG...]
    slice x1 -> x0, local copies, waits for them, and re-layouts: 1.44 us -> none  [per_device(): return (operator, xr[:, 0], xr[:, 1])]
where the time goes in v2:
time: 71.4 us; the launch traced here: 71.1 us
  Pallas kernels  69.2 us (97%)
  between operations  1.93 us (3%)
    pallas_call x1, Pallas kernels, call_kernel(): pl.pallas_call(functools.partial(kernel, groups, rows_axis), out_shape=(j...  62.4 us
    pallas_call x1, Pallas kernels, call_open(): pl.pallas_call(functools.partial(open_slots, rows_axis), out_shape=(jax.S...  6.78 us

profile of v2, /device:TPU:1, one launch (start us, length us, event | category | flops | bytes accessed | tf_op | source)
XLA Modules:
  0.0 71.1 jit_solution(4854688892952518845)
XLA Ops:
  1.9 62.4 %shard_map.103 = (s16[8,7,128,128]{3,2,1,0:T(8,128)(2,1)}, f32[8,8,128]{2,1,0:T(8,128)}, f32[8,8,128]{2,1,0:T(8,128)}) custom-call(s32[2,10240]{1,0:T(2,128)} %bitcast.4, s32[1024]{0:T(1024)} %owner.3, f32[1]{0:T(128)S(6)} %copy.11.lam_low, f32[1]{0:T(128)S(6)} %copy.12.lam_high, s32[5,40]{1,0:T(8,128)} %bitcast.5, bf16[40,5,128,128]{3,2,1,0:T(8,128)(2,1)} %a_hbm.1, ...), custom_call_target="tpu_custom_call" | custom-call | tf_op jit(solution)/shard_map/pallas_call | solution.py:354
  64.3 6.8 %shard_map.104 = (f32[8,7,128,128]{3,2,1,0:T(8,128)}, f32[8,128]{1,0:T(8,128)}, f32[8,128]{1,0:T(8,128)}) custom-call(s32[1024]{0:T(1024)} %owner.3, s16[8,7,128,128]{3,2,1,0:T(8,128)(2,1)} %get-tuple-element.6.q_ref, f32[8,8,128]{2,1,0:T(8,128)} %get-tuple-element.7.scale_ref, f32[8,8,128]{2,1,0:T(8,128)} %get-tuple-element.8.xr_ref), custom_call_target="tpu_custom_call" | custom-call | tf_op jit(solution)/shard_map/pallas_call | solution.py:420

commit v3 on v2

v3 whole, which is shorter than its diff:
```python
import functools

import jax
import jax.numpy as jnp
from jax import lax
from jax.experimental import pallas as pl
from jax.experimental.pallas import tpu as pltpu
from jax.sharding import PartitionSpec as P

MESH = pl.DeviceIdType.MESH
BLK = 128
AGG = 10
AGGS = 4
ROWS = AGG * AGGS
F32 = jnp.float32
BF16 = jnp.bfloat16
Q_MAX = 32767.0
TINY = 2.0**-110
TRAVEL = ((5, 6, 0, 1, 4, 2, 3), (3, 4, 5, 6, 0, 1, 2), (0, 1, 2, 3, 6, 5, 4), (0, 1, 6, 5, 2, 4, 3))
CUTS = ((0, 3), (3, 5), (5, 7))
DOWN = (5, 6, 2, 3, 4)
UP = (0, 1, 4, 2, 3)
PARTS = ((0, 2), (2, 3), (3, 5))


def quantised(block):
    top = jnp.maximum(jnp.max(jnp.abs(block), axis=0, keepdims=True), TINY)
    q = jnp.floor(block * (Q_MAX / top) + 0.5).astype(jnp.int32).astype(jnp.int16)
    return q, top * (1.0 / Q_MAX)


def chebyshev_terms(low, high):
    center = 0.5 * (high + low)
    radius = 0.5 * (high - low)
    sigma_ratio = center / radius
    first_rho = 1.0 / sigma_ratio
    second_rho = 1.0 / (2.0 * sigma_ratio - first_rho)
    return center, second_rho * first_rho, 2.0 * second_rho / radius


def wrapped(x, total):
    x = jnp.where(x > total // 2, x - total, x)
    return jnp.where(x < -(total // 2), x + total, x)


def write_tables(fine_total, coarse_total, first_row, base, fc, pc, skip, tbl):
    row = lax.broadcasted_iota(jnp.int32, (5, ROWS), 1)
    reach = wrapped(fc[...] - (first_row + row), fine_total)
    place = row + AGG + reach
    near = [jnp.zeros((5, ROWS), jnp.int32) for _ in range(2)]
    for p in range(ROWS + 2 * AGG):
        for q in range(2):
            near[q] = jnp.where(place == p, pc[(skip + p) // BLK, q, (skip + p) % BLK], near[q])
    agg = jnp.zeros((5, ROWS), jnp.int32)
    for k in range(1, AGGS):
        agg = agg + jnp.where(row >= k * AGG, 1, 0)
    offset = [wrapped(c - base - agg, coarse_total) + 2 for c in near]

    def pick(o, ok, first, second, none):
        got = jnp.where(ok & (offset[0] == o), first, none)
        return jnp.where(ok & (offset[1] == o), second, got)

    inside = (place >= AGG) & (place < ROWS + AGG)
    mine = 2 * (place - AGG)
    for o in range(5):
        tbl[o, 0:5, 0:ROWS] = pick(o, inside, mine, mine + 1, 2 * ROWS)
    below = (place >= 0) & (place < AGG)
    above = (place >= ROWS + AGG) & (place < ROWS + 2 * AGG)
    high = place - ROWS - AGG
    low_part = jnp.where(below & (offset[0] == 0), place, AGG)
    high_part = jnp.where(above & (offset[1] == 4), high, AGG)
    tbl[5, 0:5, 0:ROWS] = jnp.where(row < 2 * AGG, low_part, high_part)
    for n in range(2):
        from_low = pick(1 + n, below, place, place + AGG, 2 * AGG)
        from_high = pick(2 + n, above, high + AGG, high, 2 * AGG)
        tbl[6 + n, 0:5, 0:ROWS] = jnp.where(row < 2 * AGG, from_low, from_high)
    everywhere = row >= 0
    for t in range(3):
        tbl[8 + t, 0:5, 0:ROWS] = pick(t + 1, everywhere, 2 * row, 2 * row + 1, 2 * ROWS)


def kernel(
    groups, rows_axis,
    owner, lam_low, lam_high, pc_hbm, fc, a_hbm, p_hbm, p_pairs, rhs_ref,
    q_out, sc_out, xr_out,
    pc, tbl_v, tbl, a_v, p_v, lo_part, lo_all, hi_part, hi_all, pt, m_v, acc_lo, acc_hi, co, qb, sb, sq, ss, xrb, sx,
    pq_s, ps_s, pq_r, ps_r, own, halo_x, own2, halo_x2, tot,
    a_sem, p_sem, t_sem, nb_send, nb_recv, g0_send, g0_recv, g1_send, g1_recv, g2_send, g2_recv,
    gs_send, gs_recv, gx_send, gx_recv, self_sem,
):
    g = lax.axis_index("grp")
    r = lax.axis_index("row")
    device = g * rows_axis + r
    devices = groups * rows_axis
    base = device * AGGS
    last = (r + 1) // rows_axis
    nxt = ((g + last) % groups, (r + 1) % rows_axis)
    first = (rows_axis - r) // rows_axis
    prv = ((g + groups - first) % groups, (r + rows_axis - 1) % rows_axis)

    barrier = pltpu.get_barrier_semaphore()
    for target in (nxt, prv):
        pl.semaphore_signal(barrier, inc=1, device_id=target, device_id_type=MESH)
    for off in range(1, groups):
        pl.semaphore_signal(barrier, inc=1, device_id=((g + off) % groups, r), device_id_type=MESH)

    fine_total = ROWS * devices
    start = (device * ROWS + fine_total - AGG) % fine_total
    chunk = start // BLK
    pc_copies = [
        pltpu.make_async_copy(
            pc_hbm.at[:, pl.ds(pl.multiple_of(((chunk + n) % (fine_total // BLK)) * BLK, BLK), BLK)], pc.at[n], t_sem.at[n])
        for n in range(2)
    ]
    for copy in pc_copies:
        copy.start()
    p_copy = pltpu.make_async_copy(p_hbm, p_v.at[pl.ds(0, 2 * ROWS)], p_sem)
    p_copy.start()
    a_copies = [
        pltpu.make_async_copy(a_hbm.at[pl.ds(k * AGG, AGG)], a_v.at[pl.ds(k * AGG, AGG)], a_sem.at[k])
        for k in range(AGGS)
    ]
    for k in (0, 3, 1, 2):
        a_copies[k].start()

    own[...] = jnp.zeros_like(own)
    own[0:AGGS, :] = rhs_ref[...]
    tbl_v[...] = jnp.zeros_like(tbl_v)
    pl.semaphore_wait(barrier, groups + 1)

    def to_neighbour(slot, src, dst, target):
        return pltpu.make_async_remote_copy(
            src_ref=src, dst_ref=dst, send_sem=nb_send.at[slot], recv_sem=nb_recv.at[slot],
            device_id=target, device_id_type=MESH)

    last_rows = pl.ds(ROWS - AGG, AGG)
    first_rows = pl.ds(0, AGG)
    rest = pl.ds(AGG, AGG)
    p_next = (
        to_neighbour(0, p_pairs.at[last_rows, 0], lo_part.at[first_rows], nxt),
        to_neighbour(1, p_pairs.at[last_rows, 1], lo_all.at[rest], nxt),
    )
    p_prev = (
        to_neighbour(2, p_pairs.at[first_rows, 1], hi_part.at[first_rows], prv),
        to_neighbour(3, p_pairs.at[first_rows, 0], hi_all.at[rest], prv),
    )
    for n in range(2):
        p_next[n].start()
        p_prev[n].start()
    x_next = to_neighbour(4, own, halo_x.at[0], nxt)
    x_prev = to_neighbour(5, own, halo_x.at[1], prv)
    x_next.start()
    x_prev.start()

    for copy in pc_copies:
        copy.wait()
    write_tables(fine_total, AGGS * devices, device * ROWS, base, fc, pc, start % BLK, tbl_v)
    t_copy = pltpu.make_async_copy(tbl_v, tbl, t_sem.at[2])
    t_copy.start()
    zero_block = jnp.zeros((BLK, BLK), BF16)
    p_v[2 * ROWS] = zero_block
    lo_part[AGG] = zero_block
    hi_part[AGG] = zero_block
    lo_all[2 * AGG] = zero_block
    hi_all[2 * AGG] = zero_block
    co[...] = jnp.zeros_like(co)
    t_copy.wait()
    p_copy.wait()

    def turn(i, carry):
        for t in range(3):
            pt[i, t * BLK:(t + 1) * BLK, :] = p_v[tbl[8 + t, 0, i]].T
        return carry

    lax.fori_loop(0, ROWS, turn, 0)

    def gathered(ref, i, plane, entries, cols):
        return jnp.concatenate(
            [jnp.concatenate([ref[tbl[plane + o, a, i]] for o in cols], axis=1) for a in entries], axis=0)

    def local_rows(start, count, plan):
        def step(n, carry):
            i = start + n
            lhs = jnp.concatenate([a_v[i, a] for a in range(5)], axis=1)
            for cols, keep, first_col in plan:
                got = jnp.dot(lhs, gathered(p_v, i, 0, range(5), cols), preferred_element_type=F32)
                lo = (cols[0] - first_col) * BLK
                hi = (cols[-1] + 1 - first_col) * BLK
                if keep is None:
                    m_v[i, :, lo:hi] = got.astype(BF16)
                else:
                    keep[n, :, lo:hi] = got
            return carry

        lax.fori_loop(0, count, step, 0)

    def lift(k, groups_of_cols):
        lhs = jnp.concatenate([pt[k * AGG + n] for n in range(AGG)], axis=1)
        for cols in groups_of_cols:
            rhs = m_v[k * AGG:(k + 1) * AGG, :, cols[0] * BLK:(cols[-1] + 1) * BLK]
            rhs = rhs.reshape(AGG * BLK, len(cols) * BLK)
            got = jnp.dot(lhs, rhs, preferred_element_type=F32)
            for t in range(3):
                for n, o in enumerate(cols):
                    co[k + t, o - t + 2] += got[t * BLK:(t + 1) * BLK, n * BLK:(n + 1) * BLK]

    def send_partial(part, side):
        row, all_s, target = ((0, DOWN, prv), (AGGS + 1, UP, nxt))[side]
        lo, hi = PARTS[part]
        ps_s[side, part] = jnp.zeros_like(ps_s[side, part])
        for n in range(lo, hi):
            q, scale = quantised(co[row, all_s[n]])
            pq_s[side, n] = q
            ps_s[side, part, n:n + 1, :] = scale
        slot = 6 + 4 * part + 2 * side
        copies = (
            to_neighbour(slot, pq_s.at[side, pl.ds(lo, hi - lo)], pq_r.at[side, pl.ds(lo, hi - lo)], target),
            to_neighbour(slot + 1, ps_s.at[side, part], ps_r.at[side, part], target),
        )
        for copy in copies:
            copy.start()
        return copies

    def receive_partial(copies, part, side):
        row, all_s = ((AGGS, DOWN), (1, UP))[side]
        for copy in copies:
            copy.wait_recv()
        for n in range(*PARTS[part]):
            co[row, all_s[n]] += pq_r[side, n].astype(jnp.int32).astype(F32) * ps_r[side, part, n:n + 1, :]

    a_copies[0].wait()
    local_rows(0, AGG, (((0, 1), acc_lo, 0), ((2,), acc_lo, 0), ((3, 4), None, 0)))
    lift(0, ((3, 4),))
    sent = {(0, 0): send_partial(0, 0)}
    a_copies[3].wait()
    local_rows(3 * AGG, AGG, (((0, 1), None, 0), ((2, 3), acc_hi, 2), ((4,), acc_hi, 2)))
    lift(3, ((0, 1),))
    sent[0, 1] = send_partial(0, 1)
    a_copies[1].wait()
    a_copies[2].wait()
    local_rows(AGG, 2 * AGG, (((0, 1), None, 0), ((2, 3), None, 0), ((4,), None, 0)))
    lift(1, ((0, 1), (2, 3), (4,)))
    lift(2, ((0, 1), (2, 3), (4,)))

    def pack(k, places):
        for place in places:
            q, scale = quantised(co[k + 1, TRAVEL[k][place]])
            qb[k, place] = q
            sb[k, place:place + 1, :] = scale

    def owned(dest):
        k = AGGS
        for c in range(AGGS):
            k = jnp.where(owner[base + c] == dest, c, k)
        return k

    def to_owner(off, src, dst, send, recv, lo, hi):
        return pltpu.make_async_remote_copy(
            src_ref=src.at[off, pl.ds(lo, hi - lo)], dst_ref=dst.at[g, pl.ds(lo, hi - lo)],
            send_sem=send.at[off], recv_sem=recv.at[off],
            device_id=((g + off) % groups, r), device_id_type=MESH)

    def from_maker(off, src, dst, send, recv, lo, hi):
        return pltpu.make_async_remote_copy(
            src_ref=src.at[off, pl.ds(lo, hi - lo)],
            dst_ref=dst.at[(g + groups - off) % groups, pl.ds(lo, hi - lo)], send_sem=send.at[off],
            recv_sem=recv.at[off], device_id=((g + groups - off) % groups, r), device_id_type=MESH)

    order = (4, 3, 5, 2, 6, 1, 7)
    parts = (
        (sq, q_out, g0_send, g0_recv, *CUTS[0]),
        (sq, q_out, g1_send, g1_recv, *CUTS[1]),
        (sq, q_out, g2_send, g2_recv, *CUTS[2]),
    )
    scales = (ss, sc_out, gs_send, gs_recv, 0, 8)
    vectors = (sx, xr_out, gx_send, gx_recv, 0, 8)

    def repartition(part):
        lo, hi = CUTS[part]
        for off in order + (0,):
            sq[off, lo:hi] = qb[owned((g + off) % groups), lo:hi]
            if off:
                to_owner(off, *parts[part]).start()

    qb[AGGS] = jnp.zeros_like(qb[AGGS])
    sb[...] = jnp.zeros_like(sb)
    for side in range(2):
        receive_partial(sent[0, side], 0, side)
    for k in range(AGGS):
        pack(k, range(*CUTS[0]))
    repartition(0)

    def halo_rows(start, ref, plane, count, keep, keep_col, first_col):
        width = count * BLK

        def step(n, carry):
            i = start + n
            lhs = jnp.concatenate([a_v[i, a] for a in range(1, 5)], axis=1)
            got = jnp.dot(lhs, gathered(ref, i, plane, range(1, 5), range(count)), preferred_element_type=F32)
            got = got + keep[n, :, keep_col * BLK:keep_col * BLK + width]
            m_v[i, :, first_col * BLK:first_col * BLK + width] = got.astype(BF16)
            return carry

        lax.fori_loop(0, AGG, step, 0)

    p_next[0].wait_recv()
    halo_rows(0, lo_part, 5, 1, acc_lo, 0, 0)
    lift(0, ((0,),))
    sent[1, 0] = send_partial(1, 0)
    p_prev[0].wait_recv()
    halo_rows(3 * AGG, hi_part, 5, 1, acc_hi, 2, 4)
    lift(3, ((4,),))
    sent[1, 1] = send_partial(1, 1)
    lo_all[0:AGG] = lo_part[0:AGG]
    hi_all[0:AGG] = hi_part[0:AGG]
    p_next[1].wait_recv()
    halo_rows(0, lo_all, 6, 2, acc_lo, 1, 1)
    lift(0, ((1, 2),))
    sent[2, 0] = send_partial(2, 0)
    p_prev[1].wait_recv()
    halo_rows(3 * AGG, hi_all, 6, 2, acc_hi, 0, 2)
    lift(3, ((2, 3),))
    sent[2, 1] = send_partial(2, 1)

    for side in range(2):
        receive_partial(sent[1, side], 1, side)
    for k in range(AGGS):
        pack(k, range(*CUTS[1]))
    repartition(1)
    pack(1, range(*CUTS[2]))
    pack(2, range(*CUTS[2]))

    x_next.wait_recv()
    x_prev.wait_recv()
    center, old_weight, resid_weight = chebyshev_terms(
        jnp.full((1, BLK), lam_low[0], F32), jnp.full((1, BLK), lam_high[0], F32))

    def products(k, mine, halo, scale_by, of_mine, of_halo):
        total = jnp.zeros((BLK, BLK), F32)
        for s in range(7):
            c = k + s - 3
            here = 0 <= c < AGGS
            if not (of_mine if here else of_halo):
                continue
            if here:
                row = mine[c:c + 1, :]
            elif c < 0:
                row = halo[0, AGGS + c:AGGS + c + 1, :]
            else:
                row = halo[1, c - AGGS:c - AGGS + 1, :]
            if scale_by is not None:
                row = row / scale_by
            total = total + co[k + 1, s] * row
        return total

    def summed(total):
        return jnp.sum(total.T, axis=0, keepdims=True)

    own2[...] = jnp.zeros_like(own2)
    xrb[...] = jnp.zeros_like(xrb)

    def first_sweep(k):
        rhs = own[k:k + 1, :]
        x1 = rhs / center
        residual = rhs - summed(products(k, own, halo_x, center, True, True))
        x2 = x1 + old_weight * x1 + resid_weight * residual
        own2[k:k + 1, :] = x2
        xrb[k, 0:1, :] = x2

    first_sweep(1)
    first_sweep(2)
    receive_partial(sent[2, 0], 2, 0)
    first_sweep(3)
    receive_partial(sent[2, 1], 2, 1)
    first_sweep(0)
    x2_next = to_neighbour(18, own2, halo_x2.at[0], nxt)
    x2_prev = to_neighbour(19, own2, halo_x2.at[1], prv)
    x2_next.start()
    x2_prev.start()
    pack(3, range(*CUTS[2]))
    pack(0, range(*CUTS[2]))
    repartition(2)
    for off in order + (0,):
        ss[off] = sb[owned((g + off) % groups)]
        if off:
            to_owner(off, *scales).start()
    own_q = pltpu.make_async_copy(sq.at[0], q_out.at[g], self_sem.at[0])
    own_s = pltpu.make_async_copy(ss.at[0], sc_out.at[g], self_sem.at[1])
    own_q.start()
    own_s.start()
    for k in range(AGGS):
        tot[k] = products(k, own2, halo_x2, None, True, False)
    x2_next.wait_recv()
    x2_prev.wait_recv()
    for k in range(AGGS):
        total = tot[k] + products(k, own2, halo_x2, None, False, True)
        xrb[k, 1:2, :] = own[k:k + 1, :] - summed(total)
    for off in order + (0,):
        sx[off] = xrb[owned((g + off) % groups)]
        if off:
            to_owner(off, *vectors).start()
    own_x = pltpu.make_async_copy(sx.at[0], xr_out.at[g], self_sem.at[2])
    own_x.start()

    for copy in (*p_next, *p_prev, x_next, x_prev, x2_next, x2_prev):
        copy.wait_send()
    for copies in sent.values():
        for copy in copies:
            copy.wait_send()
    for off in order:
        for args in (*parts, scales, vectors):
            to_owner(off, *args).wait_send()
            from_maker(off, *args).wait_recv()
    own_q.wait()
    own_s.wait()
    own_x.wait()


def call_kernel(groups, rows_axis, owner, lam_low, lam_high, pc, fc, a, p, rhs):
    hbm = pl.BlockSpec(memory_space=pl.ANY)
    smem = pl.BlockSpec(memory_space=pltpu.SMEM)
    vmem = pl.BlockSpec(memory_space=pltpu.VMEM)
    dma = pltpu.SemaphoreType.DMA
    i16 = jnp.int16
    return pl.pallas_call(
        functools.partial(kernel, groups, rows_axis),
        out_shape=(
            jax.ShapeDtypeStruct((groups, 7, BLK, BLK), i16),
            jax.ShapeDtypeStruct((groups, 8, BLK), F32),
            jax.ShapeDtypeStruct((groups, 8, BLK), F32),
        ),
        in_specs=[smem, smem, smem, hbm, vmem, hbm, hbm, hbm, vmem],
        out_specs=(hbm, hbm, hbm),
        scratch_shapes=[
            pltpu.SMEM((2, 2, BLK), jnp.int32),
            pltpu.VMEM((11, 8, BLK), jnp.int32),
            pltpu.SMEM((11, 8, BLK), jnp.int32),
            pltpu.VMEM((ROWS, 5, BLK, BLK), BF16),
            pltpu.VMEM((2 * ROWS + 1, BLK, BLK), BF16),
            pltpu.VMEM((AGG + 1, BLK, BLK), BF16),
            pltpu.VMEM((2 * AGG + 1, BLK, BLK), BF16),
            pltpu.VMEM((AGG + 1, BLK, BLK), BF16),
            pltpu.VMEM((2 * AGG + 1, BLK, BLK), BF16),
            pltpu.VMEM((ROWS, 3 * BLK, BLK), BF16),
            pltpu.VMEM((ROWS, BLK, 5 * BLK), BF16),
            pltpu.VMEM((AGG, BLK, 3 * BLK), F32),
            pltpu.VMEM((AGG, BLK, 3 * BLK), F32),
            pltpu.VMEM((AGGS + 2, 7, BLK, BLK), F32),
            pltpu.VMEM((AGGS + 1, 7, BLK, BLK), i16),
            pltpu.VMEM((AGGS + 1, 8, BLK), F32),
            pltpu.VMEM((groups, 7, BLK, BLK), i16),
            pltpu.VMEM((groups, 8, BLK), F32),
            pltpu.VMEM((AGGS + 1, 8, BLK), F32),
            pltpu.VMEM((groups, 8, BLK), F32),
            pltpu.VMEM((2, 5, BLK, BLK), i16),
            pltpu.VMEM((2, 3, 8, BLK), F32),
            pltpu.VMEM((2, 5, BLK, BLK), i16),
            pltpu.VMEM((2, 3, 8, BLK), F32),
            pltpu.VMEM((8, BLK), F32),
            pltpu.VMEM((2, 8, BLK), F32),
            pltpu.VMEM((8, BLK), F32),
            pltpu.VMEM((2, 8, BLK), F32),
            pltpu.VMEM((AGGS, BLK, BLK), F32),
            dma((AGGS,)), dma, dma((3,)), dma((20,)), dma((20,)),
            dma((groups,)), dma((groups,)),
            dma((groups,)), dma((groups,)), dma((groups,)), dma((groups,)),
            dma((groups,)), dma((groups,)), dma((groups,)), dma((groups,)),
            dma((3,)),
        ],
        compiler_params=pltpu.CompilerParams(
            collective_id=0, has_side_effects=True, vmem_limit_bytes=56 << 20),
    )(owner, lam_low, lam_high, pc, fc, a, p.reshape(2 * ROWS, BLK, BLK), p, rhs)


def open_slots(groups, rows_axis, owner, q_hbm, scale, xr, out_hbm, x_ref, r_ref, q_v, o_v, in_sem, out_sem):
    g = lax.axis_index("grp")
    r = lax.axis_index("row")

    def arrive(n):
        return pltpu.make_async_copy(q_hbm.at[n], q_v.at[n], in_sem.at[n])

    def leave(n):
        return pltpu.make_async_copy(o_v.at[n], out_hbm.at[n], out_sem.at[n])

    for n in range(groups):
        arrive(n).start()
    for n in range(groups):
        x_ref[n:n + 1, :] = xr[n, 0:1, :]
        r_ref[n:n + 1, :] = xr[n, 1:2, :]

    def step(n, carry):
        first = (n * rows_axis + r) * AGGS
        places = [TRAVEL[0].index(s) for s in range(7)]
        for k in range(1, AGGS):
            mine = owner[first + k] == g
            places = [jnp.where(mine, TRAVEL[k].index(s), places[s]) for s in range(7)]
        arrive(n).wait()
        for s in range(7):
            o_v[n, s] = q_v[n, places[s]].astype(jnp.int32).astype(F32) * scale[n, pl.ds(places[s], 1), :]
        leave(n).start()
        return carry

    lax.fori_loop(0, groups, step, 0)
    for n in range(groups):
        leave(n).wait()


def call_open(groups, rows_axis, owner, q, scale, xr):
    hbm = pl.BlockSpec(memory_space=pl.ANY)
    vmem = pl.BlockSpec(memory_space=pltpu.VMEM)
    return pl.pallas_call(
        functools.partial(open_slots, groups, rows_axis),
        out_shape=(
            jax.ShapeDtypeStruct((groups, 7, BLK, BLK), F32),
            jax.ShapeDtypeStruct((groups, BLK), F32),
            jax.ShapeDtypeStruct((groups, BLK), F32),
        ),
        in_specs=[pl.BlockSpec(memory_space=pltpu.SMEM), hbm, vmem, vmem],
        out_specs=(hbm, vmem, vmem),
        scratch_shapes=[
            pltpu.VMEM((groups, 7, BLK, BLK), jnp.int16),
            pltpu.VMEM((groups, 7, BLK, BLK), F32),
            pltpu.SemaphoreType.DMA((groups,)),
            pltpu.SemaphoreType.DMA((groups,)),
        ],
    )(owner, q, scale, xr)


def per_device(
    fine_cols, fine_blocks, prolong_cols, prolong_blocks, agg_owner, coarse_rhs, lam_low, lam_high
):
    groups = lax.axis_size("grp")
    rows_axis = lax.axis_size("row")
    q, scale, xr = call_kernel(
        groups, rows_axis, agg_owner, lam_low, lam_high, prolong_cols.T, fine_cols.T, fine_blocks, prolong_blocks,
        coarse_rhs)
    return call_open(groups, rows_axis, agg_owner, q, scale, xr)


def solution(mesh):
    return jax.shard_map(
        per_device,
        mesh=mesh,
        in_specs=(
            P(("grp", "row"), None),
            P(("grp", "row"), None, None, None),
            P(),
            P(("grp", "row"), None, None, None),
            P(),
            P(("grp", "row"), None),
            P(),
            P(),
        ),
        out_specs=(
            P(("grp", "row"), None, None, None),
            P(("grp", "row"), None),
            P(("grp", "row"), None),
        ),
        check_vma=False,
    )
```

time: 71.4 us -> 65.1 us (0.912)
  Pallas kernels: 69.2 us -> 62.9 us
    pallas_call x1, Pallas kernels: 62.4 us -> 58.6 us  [call_kernel(): pl.pallas_call(functools.partial(kernel, groups, rows_axis), out_shape=(j...]
    pallas_call x1, Pallas kernels: 6.78 us -> 4.33 us  [call_open(): pl.pallas_call(functools.partial(open_slots, groups, rows_axis), out_shap...]
where the time goes in v3:
time: 65.1 us; the launch traced here: 64.9 us
  Pallas kernels  62.9 us (97%)
  between operations  1.93 us (3%)
    pallas_call x1, Pallas kernels, call_kernel(): pl.pallas_call(functools.partial(kernel, groups, rows_axis), out_shape=(j...  58.6 us
    pallas_call x1, Pallas kernels, call_open(): pl.pallas_call(functools.partial(open_slots, groups, rows_axis), out_shap...  4.33 us

profile of v3, /device:TPU:1, one launch (start us, length us, event | category | flops | bytes accessed | tf_op | source)
XLA Modules:
  0.0 64.9 jit_solution(8039569334525776901)
XLA Ops:
  1.9 58.6 %shard_map.103 = (s16[8,7,128,128]{3,2,1,0:T(8,128)(2,1)}, f32[8,8,128]{2,1,0:T(8,128)}, f32[8,8,128]{2,1,0:T(8,128)}) custom-call(s32[1024]{0:T(1024)} %owner.3, f32[1]{0:T(128)S(6)} %copy.11.lam_low, f32[1]{0:T(128)S(6)} %copy.12.lam_high, s32[2,10240]{1,0:T(2,128)} %bitcast.4, s32[5,40]{1,0:T(8,128)} %bitcast.5, bf16[40,5,128,128]{3,2,1,0:T(8,128)(2,1)} %a_hbm.1, ...), custom_call_target="tpu_custom_call" | custom-call | tf_op jit(solution)/shard_map/pallas_call | solution.py:425
  60.6 4.3 %shard_map.104 = (f32[8,7,128,128]{3,2,1,0:T(8,128)}, f32[8,128]{1,0:T(8,128)}, f32[8,128]{1,0:T(8,128)}) custom-call(s32[1024]{0:T(1024)} %owner.3, s16[8,7,128,128]{3,2,1,0:T(8,128)(2,1)} %get-tuple-element.6.q_hbm, f32[8,8,128]{2,1,0:T(8,128)} %get-tuple-element.7.scale, f32[8,8,128]{2,1,0:T(8,128)} %get-tuple-element.8.xr), custom_call_target="tpu_custom_call" | custom-call | tf_op jit(solution)/shard_map/pallas_call | solution.py:511

commit v4 on v3

--- a/solution.py
+++ b/solution.py
@@ -16,6 +16,7 @@
 BF16 = jnp.bfloat16
 Q_MAX = 32767.0
 TINY = 2.0**-110
+TOGETHER = 5
 TRAVEL = ((5, 6, 0, 1, 4, 2, 3), (3, 4, 5, 6, 0, 1, 2), (0, 1, 2, 3, 6, 5, 4), (0, 1, 6, 5, 2, 4, 3))
 CUTS = ((0, 3), (3, 5), (5, 7))
 DOWN = (5, 6, 2, 3, 4)
@@ -144,9 +145,8 @@
         to_neighbour(2, p_pairs.at[first_rows, 1], hi_part.at[first_rows], prv),
         to_neighbour(3, p_pairs.at[first_rows, 0], hi_all.at[rest], prv),
     )
-    for n in range(2):
-        p_next[n].start()
-        p_prev[n].start()
+    p_next[0].start()
+    p_prev[0].start()
     x_next = to_neighbour(4, own, halo_x.at[0], nxt)
     x_prev = to_neighbour(5, own, halo_x.at[1], prv)
     x_next.start()
@@ -167,19 +167,26 @@
     t_copy.wait()
     p_copy.wait()
 
-    def turn(i, carry):
+    def for_rows(count, body):
+        def step(n, carry):
+            for m in range(TOGETHER):
+                body(n * TOGETHER + m)
+            return carry
+
+        lax.fori_loop(0, count // TOGETHER, step, 0)
+
+    def turn(i):
         for t in range(3):
             pt[i, t * BLK:(t + 1) * BLK, :] = p_v[tbl[8 + t, 0, i]].T
-        return carry
-
-    lax.fori_loop(0, ROWS, turn, 0)
+
+    for_rows(ROWS, turn)
 
     def gathered(ref, i, plane, entries, cols):
         return jnp.concatenate(
             [jnp.concatenate([ref[tbl[plane + o, a, i]] for o in cols], axis=1) for a in entries], axis=0)
 
     def local_rows(start, count, plan):
-        def step(n, carry):
+        def body(n):
             i = start + n
             lhs = jnp.concatenate([a_v[i, a] for a in range(5)], axis=1)
             for cols, keep, first_col in plan:
@@ -190,9 +197,8 @@
                     m_v[i, :, lo:hi] = got.astype(BF16)
                 else:
                     keep[n, :, lo:hi] = got
-            return carry
-
-        lax.fori_loop(0, count, step, 0)
+
+        for_rows(count, body)
 
     def lift(k, groups_of_cols):
         lhs = jnp.concatenate([pt[k * AGG + n] for n in range(AGG)], axis=1)
@@ -236,6 +242,10 @@
     local_rows(3 * AGG, AGG, (((0, 1), None, 0), ((2, 3), acc_hi, 2), ((4,), acc_hi, 2)))
     lift(3, ((0, 1),))
     sent[0, 1] = send_partial(0, 1)
+    p_next[0].wait_send()
+    p_next[1].start()
+    p_prev[0].wait_send()
+    p_prev[1].start()
     a_copies[1].wait()
     a_copies[2].wait()
     local_rows(AGG, 2 * AGG, (((0, 1), None, 0), ((2, 3), None, 0), ((4,), None, 0)))
@@ -293,15 +303,14 @@
     def halo_rows(start, ref, plane, count, keep, keep_col, first_col):
         width = count * BLK
 
-        def step(n, carry):
+        def body(n):
             i = start + n
             lhs = jnp.concatenate([a_v[i, a] for a in range(1, 5)], axis=1)
             got = jnp.dot(lhs, gathered(ref, i, plane, range(1, 5), range(count)), preferred_element_type=F32)
             got = got + keep[n, :, keep_col * BLK:keep_col * BLK + width]
             m_v[i, :, first_col * BLK:first_col * BLK + width] = got.astype(BF16)
-            return carry
-
-        lax.fori_loop(0, AGG, step, 0)
+
+        for_rows(AGG, body)
 
     p_next[0].wait_recv()
     halo_rows(0, lo_part, 5, 1, acc_lo, 0, 0)
@@ -402,7 +411,7 @@
     own_x = pltpu.make_async_copy(sx.at[0], xr_out.at[g], self_sem.at[2])
     own_x.start()
 
-    for copy in (*p_next, *p_prev, x_next, x_prev, x2_next, x2_prev):
+    for copy in (p_next[1], p_prev[1], x_next, x_prev, x2_next, x2_prev):
         copy.wait_send()
     for copies in sent.values():
         for copy in copies:

time: 65.1 us -> 58.7 us (0.902)
  Pallas kernels: 62.9 us -> 56.6 us
    pallas_call x1, Pallas kernels: 58.6 us -> 52.2 us  [call_kernel(): pl.pallas_call(functools.partial(kernel, groups, rows_axis), out_shape=(j...]
where the time goes in v4:
time: 58.7 us; the launch traced here: 58.5 us
  Pallas kernels  56.6 us (96%)
  between operations  1.93 us (3%)
    pallas_call x1, Pallas kernels, call_kernel(): pl.pallas_call(functools.partial(kernel, groups, rows_axis), out_shape=(j...  52.2 us
    pallas_call x1, Pallas kernels, call_open(): pl.pallas_call(functools.partial(open_slots, groups, rows_axis), out_shap...  4.33 us

profile of v4, /device:TPU:1, one launch (start us, length us, event | category | flops | bytes accessed | tf_op | source)
XLA Modules:
  0.0 58.5 jit_solution(4234411109410378118)
XLA Ops:
  1.9 52.2 %shard_map.103 = (s16[8,7,128,128]{3,2,1,0:T(8,128)(2,1)}, f32[8,8,128]{2,1,0:T(8,128)}, f32[8,8,128]{2,1,0:T(8,128)}) custom-call(s32[1024]{0:T(1024)} %owner.3, f32[1]{0:T(128)S(6)} %copy.11.lam_low, f32[1]{0:T(128)S(6)} %copy.12.lam_high, s32[2,10240]{1,0:T(2,128)} %bitcast.4, s32[5,40]{1,0:T(8,128)} %bitcast.5, bf16[40,5,128,128]{3,2,1,0:T(8,128)(2,1)} %a_hbm.1, ...), custom_call_target="tpu_custom_call" | custom-call | tf_op jit(solution)/shard_map/pallas_call | solution.py:434
  54.2 4.3 %shard_map.104 = (f32[8,7,128,128]{3,2,1,0:T(8,128)}, f32[8,128]{1,0:T(8,128)}, f32[8,128]{1,0:T(8,128)}) custom-call(s32[1024]{0:T(1024)} %owner.3, s16[8,7,128,128]{3,2,1,0:T(8,128)(2,1)} %get-tuple-element.6.q_hbm, f32[8,8,128]{2,1,0:T(8,128)} %get-tuple-element.7.scale, f32[8,8,128]{2,1,0:T(8,128)} %get-tuple-element.8.xr), custom_call_target="tpu_custom_call" | custom-call | tf_op jit(solution)/shard_map/pallas_call | solution.py:520

commit v5 on v4

--- a/solution.py
+++ b/solution.py
@@ -82,9 +82,9 @@
 
 def kernel(
     groups, rows_axis,
-    owner, lam_low, lam_high, pc_hbm, fc, a_hbm, p_hbm, p_pairs, rhs_ref,
+    owner_hbm, low_hbm, high_hbm, pc_hbm, fc_hbm, a_hbm, p_hbm, p_pairs, rhs_hbm,
     q_out, sc_out, xr_out,
-    pc, tbl_v, tbl, a_v, p_v, lo_part, lo_all, hi_part, hi_all, pt, m_v, acc_lo, acc_hi, co, qb, sb, sq, ss, xrb, sx,
+    owner, lam_low, lam_high, fc, rhs_v, small_sem, pc, tbl_v, tbl, a_v, p_v, lo_part, lo_all, hi_part, hi_all, pt, m_v, acc_lo, acc_hi, co, qb, sb, sq, ss, xrb, sx,
     pq_s, ps_s, pq_r, ps_r, own, halo_x, own2, halo_x2, tot,
     a_sem, p_sem, t_sem, nb_send, nb_recv, g0_send, g0_recv, g1_send, g1_recv, g2_send, g2_recv,
     gs_send, gs_recv, gx_send, gx_recv, self_sem,
@@ -113,7 +113,12 @@
             pc_hbm.at[:, pl.ds(pl.multiple_of(((chunk + n) % (fine_total // BLK)) * BLK, BLK), BLK)], pc.at[n], t_sem.at[n])
         for n in range(2)
     ]
-    for copy in pc_copies:
+    small = [
+        pltpu.make_async_copy(src, dst, small_sem.at[n])
+        for n, (src, dst) in enumerate(
+            ((rhs_hbm, rhs_v), (fc_hbm, fc), (owner_hbm, owner), (low_hbm, lam_low), (high_hbm, lam_high)))
+    ]
+    for copy in (*pc_copies, *small):
         copy.start()
     p_copy = pltpu.make_async_copy(p_hbm, p_v.at[pl.ds(0, 2 * ROWS)], p_sem)
     p_copy.start()
@@ -124,8 +129,6 @@
     for k in (0, 3, 1, 2):
         a_copies[k].start()
 
-    own[...] = jnp.zeros_like(own)
-    own[0:AGGS, :] = rhs_ref[...]
     tbl_v[...] = jnp.zeros_like(tbl_v)
     pl.semaphore_wait(barrier, groups + 1)
 
@@ -147,18 +150,22 @@
     )
     p_next[0].start()
     p_prev[0].start()
+    small[0].wait()
+    own[...] = jnp.zeros_like(own)
+    own[0:AGGS, :] = rhs_v[...]
     x_next = to_neighbour(4, own, halo_x.at[0], nxt)
     x_prev = to_neighbour(5, own, halo_x.at[1], prv)
     x_next.start()
     x_prev.start()
 
-    for copy in pc_copies:
+    for copy in (*pc_copies, *small[1:]):
         copy.wait()
     write_tables(fine_total, AGGS * devices, device * ROWS, base, fc, pc, start % BLK, tbl_v)
     t_copy = pltpu.make_async_copy(tbl_v, tbl, t_sem.at[2])
     t_copy.start()
     zero_block = jnp.zeros((BLK, BLK), BF16)
     p_v[2 * ROWS] = zero_block
+    pt[2 * ROWS] = zero_block
     lo_part[AGG] = zero_block
     hi_part[AGG] = zero_block
     lo_all[2 * AGG] = zero_block
@@ -176,8 +183,8 @@
         lax.fori_loop(0, count // TOGETHER, step, 0)
 
     def turn(i):
-        for t in range(3):
-            pt[i, t * BLK:(t + 1) * BLK, :] = p_v[tbl[8 + t, 0, i]].T
+        for q in range(2):
+            pt[2 * i + q] = p_v[2 * i + q].T
 
     for_rows(ROWS, turn)
 
@@ -201,7 +208,8 @@
         for_rows(count, body)
 
     def lift(k, groups_of_cols):
-        lhs = jnp.concatenate([pt[k * AGG + n] for n in range(AGG)], axis=1)
+        lhs = jnp.concatenate(
+            [jnp.concatenate([pt[tbl[8 + t, 0, k * AGG + n]] for n in range(AGG)], axis=1) for t in range(3)], axis=0)
         for cols in groups_of_cols:
             rhs = m_v[k * AGG:(k + 1) * AGG, :, cols[0] * BLK:(cols[-1] + 1) * BLK]
             rhs = rhs.reshape(AGG * BLK, len(cols) * BLK)
@@ -235,20 +243,22 @@
             co[row, all_s[n]] += pq_r[side, n].astype(jnp.int32).astype(F32) * ps_r[side, part, n:n + 1, :]
 
     a_copies[0].wait()
-    local_rows(0, AGG, (((0, 1), acc_lo, 0), ((2,), acc_lo, 0), ((3, 4), None, 0)))
+    local_rows(0, AGG, (((3, 4), None, 0),))
     lift(0, ((3, 4),))
     sent = {(0, 0): send_partial(0, 0)}
     a_copies[3].wait()
-    local_rows(3 * AGG, AGG, (((0, 1), None, 0), ((2, 3), acc_hi, 2), ((4,), acc_hi, 2)))
+    local_rows(3 * AGG, AGG, (((0, 1), None, 0),))
     lift(3, ((0, 1),))
     sent[0, 1] = send_partial(0, 1)
+    inner = (((0, 1), None, 0), ((2, 3), None, 0), ((4,), None, 0))
+    a_copies[1].wait()
+    local_rows(AGG, AGG, inner)
     p_next[0].wait_send()
     p_next[1].start()
     p_prev[0].wait_send()
     p_prev[1].start()
-    a_copies[1].wait()
     a_copies[2].wait()
-    local_rows(AGG, 2 * AGG, (((0, 1), None, 0), ((2, 3), None, 0), ((4,), None, 0)))
+    local_rows(2 * AGG, AGG, inner)
     lift(1, ((0, 1), (2, 3), (4,)))
     lift(2, ((0, 1), (2, 3), (4,)))
 
@@ -299,6 +309,8 @@
     for k in range(AGGS):
         pack(k, range(*CUTS[0]))
     repartition(0)
+    local_rows(0, AGG, (((0, 1), acc_lo, 0), ((2,), acc_lo, 0)))
+    local_rows(3 * AGG, AGG, (((2, 3), acc_hi, 2), ((4,), acc_hi, 2)))
 
     def halo_rows(start, ref, plane, count, keep, keep_col, first_col):
         width = count * BLK
@@ -427,8 +439,6 @@
 
 def call_kernel(groups, rows_axis, owner, lam_low, lam_high, pc, fc, a, p, rhs):
     hbm = pl.BlockSpec(memory_space=pl.ANY)
-    smem = pl.BlockSpec(memory_space=pltpu.SMEM)
-    vmem = pl.BlockSpec(memory_space=pltpu.VMEM)
     dma = pltpu.SemaphoreType.DMA
     i16 = jnp.int16
     return pl.pallas_call(
@@ -438,9 +448,15 @@
             jax.ShapeDtypeStruct((groups, 8, BLK), F32),
             jax.ShapeDtypeStruct((groups, 8, BLK), F32),
         ),
-        in_specs=[smem, smem, smem, hbm, vmem, hbm, hbm, hbm, vmem],
+        in_specs=[hbm] * 9,
         out_specs=(hbm, hbm, hbm),
         scratch_shapes=[
+            pltpu.SMEM(owner.shape, jnp.int32),
+            pltpu.SMEM((1,), F32),
+            pltpu.SMEM((1,), F32),
+            pltpu.VMEM((5, ROWS), jnp.int32),
+            pltpu.VMEM((AGGS, BLK), F32),
+            dma((5,)),
             pltpu.SMEM((2, 2, BLK), jnp.int32),
             pltpu.VMEM((11, 8, BLK), jnp.int32),
             pltpu.SMEM((11, 8, BLK), jnp.int32),
@@ -450,7 +466,7 @@
             pltpu.VMEM((2 * AGG + 1, BLK, BLK), BF16),
             pltpu.VMEM((AGG + 1, BLK, BLK), BF16),
             pltpu.VMEM((2 * AGG + 1, BLK, BLK), BF16),
-            pltpu.VMEM((ROWS, 3 * BLK, BLK), BF16),
+            pltpu.VMEM((2 * ROWS + 1, BLK, BLK), BF16),
             pltpu.VMEM((ROWS, BLK, 5 * BLK), BF16),
             pltpu.VMEM((AGG, BLK, 3 * BLK), F32),
             pltpu.VMEM((AGG, BLK, 3 * BLK), F32),

time: 58.7 us -> 56.8 us (0.968)
  Pallas kernels: 56.6 us -> 54.7 us
    pallas_call x1, Pallas kernels: 52.2 us -> 50.3 us  [call_kernel(): pl.pallas_call(functools.partial(kernel, groups, rows_axis), out_shape=(j...]
where the time goes in v5:
time: 56.8 us; the launch traced here: 56.6 us
  Pallas kernels  54.7 us (96%)
  between operations  1.93 us (3%)
    pallas_call x1, Pallas kernels, call_kernel(): pl.pallas_call(functools.partial(kernel, groups, rows_axis), out_shape=(j...  50.3 us
    pallas_call x1, Pallas kernels, call_open(): pl.pallas_call(functools.partial(open_slots, groups, rows_axis), out_shap...  4.33 us

profile of v5, /device:TPU:1, one launch (start us, length us, event | category | flops | bytes accessed | tf_op | source)
XLA Modules:
  0.0 56.6 jit_solution(9549960409497999597)
XLA Ops:
  1.9 50.3 %shard_map.103 = (s16[8,7,128,128]{3,2,1,0:T(8,128)(2,1)}, f32[8,8,128]{2,1,0:T(8,128)}, f32[8,8,128]{2,1,0:T(8,128)}) custom-call(s32[1024]{0:T(1024)} %owner.1, f32[1]{0:T(128)S(6)} %copy.11.low_hbm, f32[1]{0:T(128)S(6)} %copy.12.high_hbm, s32[2,10240]{1,0:T(2,128)} %bitcast.4, s32[5,40]{1,0:T(8,128)} %bitcast.5, bf16[40,5,128,128]{3,2,1,0:T(8,128)(2,1)} %a_hbm.1, ...), custom_call_target="tpu_custom_call" | custom-call | tf_op jit(solution)/shard_map/pallas_call | solution.py:444
  52.3 4.3 %shard_map.104 = (f32[8,7,128,128]{3,2,1,0:T(8,128)}, f32[8,128]{1,0:T(8,128)}, f32[8,128]{1,0:T(8,128)}) custom-call(s32[1024]{0:T(1024)} %owner.1, s16[8,7,128,128]{3,2,1,0:T(8,128)(2,1)} %get-tuple-element.6.q_hbm, f32[8,8,128]{2,1,0:T(8,128)} %get-tuple-element.7.scale, f32[8,8,128]{2,1,0:T(8,128)} %get-tuple-element.8.xr), custom_call_target="tpu_custom_call" | custom-call | tf_op jit(solution)/shard_map/pallas_call | solution.py:536

commit v6 on v5

--- a/solution.py
+++ b/solution.py
@@ -497,7 +497,10 @@
     )(owner, lam_low, lam_high, pc, fc, a, p.reshape(2 * ROWS, BLK, BLK), p, rhs)
 
 
-def open_slots(groups, rows_axis, owner, q_hbm, scale, xr, out_hbm, x_ref, r_ref, q_v, o_v, in_sem, out_sem):
+def open_slots(
+    groups, rows_axis, owner_hbm, q_hbm, scale_hbm, xr_hbm, out_hbm, x_hbm, r_hbm,
+    owner, scale, xr, x_v, r_v, q_v, o_v, in_sem, out_sem, small_sem,
+):
     g = lax.axis_index("grp")
     r = lax.axis_index("row")
 
@@ -507,11 +510,18 @@
     def leave(n):
         return pltpu.make_async_copy(o_v.at[n], out_hbm.at[n], out_sem.at[n])
 
+    small = [
+        pltpu.make_async_copy(src, dst, small_sem.at[n])
+        for n, (src, dst) in enumerate(
+            ((owner_hbm, owner), (scale_hbm, scale), (xr_hbm, xr), (x_v, x_hbm), (r_v, r_hbm)))
+    ]
+    small[0].start()
+    small[1].start()
     for n in range(groups):
         arrive(n).start()
-    for n in range(groups):
-        x_ref[n:n + 1, :] = xr[n, 0:1, :]
-        r_ref[n:n + 1, :] = xr[n, 1:2, :]
+    small[2].start()
+    small[0].wait()
+    small[1].wait()
 
     def step(n, carry):
         first = (n * rows_axis + r) * AGGS
@@ -526,13 +536,20 @@
         return carry
 
     lax.fori_loop(0, groups, step, 0)
+    small[2].wait()
+    for n in range(groups):
+        x_v[n:n + 1, :] = xr[n, 0:1, :]
+        r_v[n:n + 1, :] = xr[n, 1:2, :]
+    small[3].start()
+    small[4].start()
+    small[3].wait()
+    small[4].wait()
     for n in range(groups):
         leave(n).wait()
 
 
 def call_open(groups, rows_axis, owner, q, scale, xr):
     hbm = pl.BlockSpec(memory_space=pl.ANY)
-    vmem = pl.BlockSpec(memory_space=pltpu.VMEM)
     return pl.pallas_call(
         functools.partial(open_slots, groups, rows_axis),
         out_shape=(
@@ -540,13 +557,19 @@
             jax.ShapeDtypeStruct((groups, BLK), F32),
             jax.ShapeDtypeStruct((groups, BLK), F32),
         ),
-        in_specs=[pl.BlockSpec(memory_space=pltpu.SMEM), hbm, vmem, vmem],
-        out_specs=(hbm, vmem, vmem),
+        in_specs=[hbm] * 4,
+        out_specs=(hbm,) * 3,
         scratch_shapes=[
+            pltpu.SMEM(owner.shape, jnp.int32),
+            pltpu.VMEM((groups, 8, BLK), F32),
+            pltpu.VMEM((groups, 8, BLK), F32),
+            pltpu.VMEM((groups, BLK), F32),
+            pltpu.VMEM((groups, BLK), F32),
             pltpu.VMEM((groups, 7, BLK, BLK), jnp.int16),
             pltpu.VMEM((groups, 7, BLK, BLK), F32),
             pltpu.SemaphoreType.DMA((groups,)),
             pltpu.SemaphoreType.DMA((groups,)),
+            pltpu.SemaphoreType.DMA((5,)),
         ],
     )(owner, q, scale, xr)
 

time: 56.8 us -> 55.7 us (0.981)
  Pallas kernels: 54.7 us -> 53.7 us
    pallas_call x1, Pallas kernels: 4.33 us -> 3.35 us  [call_open(): pl.pallas_call(functools.partial(open_slots, groups, rows_axis), out_shap...]
where the time goes in v6:
time: 55.7 us; the launch traced here: 55.6 us
  Pallas kernels  53.7 us (96%)
  between operations  1.93 us (3%)
    pallas_call x1, Pallas kernels, call_kernel(): pl.pallas_call(functools.partial(kernel, groups, rows_axis), out_shape=(j...  50.3 us
    pallas_call x1, Pallas kernels, call_open(): pl.pallas_call(functools.partial(open_slots, groups, rows_axis), out_shap...  3.35 us

profile of v6, /device:TPU:1, one launch (start us, length us, event | category | flops | bytes accessed | tf_op | source)
XLA Modules:
  0.0 55.6 jit_solution(1772989010612437453)
XLA Ops:
  1.9 50.3 %shard_map.103 = (s16[8,7,128,128]{3,2,1,0:T(8,128)(2,1)}, f32[8,8,128]{2,1,0:T(8,128)}, f32[8,8,128]{2,1,0:T(8,128)}) custom-call(s32[1024]{0:T(1024)} %owner_hbm.3, f32[1]{0:T(128)S(6)} %copy.11.low_hbm, f32[1]{0:T(128)S(6)} %copy.12.high_hbm, s32[2,10240]{1,0:T(2,128)} %bitcast.4, s32[5,40]{1,0:T(8,128)} %bitcast.5, bf16[40,5,128,128]{3,2,1,0:T(8,128)(2,1)} %a_hbm.1, ...), custom_call_target="tpu_custom_call" | custom-call | tf_op jit(solution)/shard_map/pallas_call | solution.py:444
  52.3 3.4 %shard_map.104 = (f32[8,7,128,128]{3,2,1,0:T(8,128)}, f32[8,128]{1,0:T(8,128)}, f32[8,128]{1,0:T(8,128)}) custom-call(s32[1024]{0:T(1024)} %owner_hbm.3, s16[8,7,128,128]{3,2,1,0:T(8,128)(2,1)} %get-tuple-element.6.q_hbm, f32[8,8,128]{2,1,0:T(8,128)} %get-tuple-element.7.scale_hbm, f32[8,8,128]{2,1,0:T(8,128)} %get-tuple-element.8.xr_hbm), custom_call_target="tpu_custom_call" | custom-call | tf_op jit(solution)/shard_map/pallas_call | solution.py:553
